TPU v7x, 1024 devices: a whole 4x8x16 slice. The times are simulated.
1024 devices in a mesh: cell: 64 (over y, x, core), mem: 16 (over z).
Axes of the slice: x: 4, y: 8, z: 16, core: 2. Of those that a mesh axis runs over, the one named last changes fastest.
Arguments:
- state: bfloat16 [128, 1048576], P('mem', 'cell'), may hold values from -6 to 6
- obs_value: float32 [131072], P('cell'), may hold values from -6 to 6
- obs_error: float32 [131072], P('cell'), may hold values from 0.25 to 1
- obs_cell: int32 [131072], P('cell'), may hold values from 0 to 1023
- obs_count: int32 [1024], P('cell'), may hold values from 32 to 128, as said below
- obs_noise: int32 [131072], P('cell'), may hold values from 0 to 511
- noise_table: float32 [128, 512], P('mem'), may hold values from -6 to 6
Outputs:
- analysis: bfloat16 [128, 1048576], P('mem', 'cell')
Inputs may be any that keep to these rules, and one draw needn't show every extreme that they name: `obs_count`: some tile has all 128 slots live in every draw.
All inputs are finite; a program needn't handle non-finite values.
Results may differ from a plain program's by a relative error of at most 0.0062.
Values may be sent and summed in bfloat16 or wider, within the bound.
No kernel may reach another device: no remote copies, remote signals or barrier semaphores. Data moves between devices by JAX's collectives and lax.ppermute only.
A program may use at most 32 MiB of HBM per device.

v0:
```python
import jax
import jax.numpy as jnp
from jax import lax
from jax.sharding import PartitionSpec as P

MEMBERS = 128
C_TILE = 1024
OBS_CAP = 128
NOISE = 512
LOCALIZE = 1024


def copy_for_each(x, axis):
    devices = lax.axis_size(axis)
    return lax.all_to_all(jnp.broadcast_to(x[None], (devices, *x.shape)), axis, 0, 0, tiled=True)


def over_copies(x, axis):
    return copy_for_each(x, axis).sum(axis=0)


def packed_total(arrays, axis):
    line, at, finished = (jnp.concatenate([a.reshape(-1) for a in arrays]), 0, [])
    running = over_copies(line, axis)
    for a in arrays:
        finished.append(running[at : at + a.size].reshape(a.shape))
        at += a.size
    return tuple(finished)


def with_halo(block, sides, width):
    for axis, dim in sides:
        count = lax.axis_size(axis)
        forward = [(i, i + 1) for i in range(count - 1)]
        backward = [(target, source) for source, target in forward]
        low = lax.ppermute(
            lax.slice_in_dim(block, block.shape[dim] - width, None, axis=dim), axis, forward
        )
        high = lax.ppermute(lax.slice_in_dim(block, 0, width, axis=dim), axis, backward)
        block = jnp.concatenate([low, block, high], axis=dim)
    return block


def side_by_side(arrays, axis, dim, along):
    both = jnp.concatenate(arrays, axis=along)
    result, at, finished = (lax.all_gather(both, axis, axis=dim, tiled=True), 0, [])
    for a in arrays:
        finished.append(lax.slice_in_dim(result, at, at + a.shape[along], axis=along))
        at += a.shape[along]
    return tuple(finished)


def three_tiles(window, tiles):
    lead = window.shape[:-1]
    blocks = window.reshape(lead + (tiles + 2, OBS_CAP))
    return jnp.concatenate(
        [blocks[..., 0:tiles, :], blocks[..., 1 : tiles + 1, :], blocks[..., 2 : tiles + 2, :]],
        axis=-1,
    )


def tapered(cell_pos, win_pos, covariance):
    ratio = jnp.abs(cell_pos[..., :, None] - win_pos[..., None, :]) / LOCALIZE
    inner = 1.0 - ratio * ratio
    tapering = jnp.where(ratio < 1.0, inner * inner, 0.0)
    return (tapering * covariance).astype(jnp.bfloat16)


def body(state, obs_value, obs_error, obs_cell, obs_count, obs_noise, noise_table):
    mem_dev, cell_count = state.shape
    tiles = cell_count // C_TILE
    slot_count = obs_value.shape[0]
    base = lax.axis_index("cell") * cell_count
    live_mask = (
        (lax.iota(jnp.int32, OBS_CAP)[None, :] < obs_count[:, None])
        .astype(jnp.float32)
        .reshape(slot_count)
    )
    local_cell = lax.iota(jnp.int32, slot_count) // OBS_CAP * C_TILE + obs_cell
    state_f32 = state.astype(jnp.float32)
    at_obs = jnp.take(state_f32, local_cell, axis=1)
    noise_pick = (lax.iota(jnp.int32, NOISE)[:, None] == obs_noise[None, :]).astype(jnp.float32)
    perturb = jnp.dot(noise_table, noise_pick, precision=lax.Precision.HIGHEST)
    sum_state, sum_square = packed_total(
        (jnp.sum(state_f32, axis=0), jnp.sum(at_obs * at_obs, axis=0)), "mem"
    )
    ens_mean = sum_state / MEMBERS
    anomaly = (state_f32 - ens_mean).astype(jnp.bfloat16)
    carried = jnp.take(anomaly, local_cell, axis=1) * live_mask.astype(jnp.bfloat16)
    mean_at = jnp.take(ens_mean, local_cell)
    spread = (sum_square - MEMBERS * mean_at * mean_at) / (MEMBERS - 1)
    weight_obs = 1.0 / (spread + obs_error)
    innovation = (
        (obs_value + jnp.sqrt(obs_error) * perturb - at_obs) * weight_obs * live_mask
    ).astype(jnp.bfloat16)
    position = (base + local_cell).astype(jnp.float32)
    payload = jnp.concatenate(
        [carried.astype(jnp.float32), innovation.astype(jnp.float32), position[None, :]], axis=0
    )
    window = with_halo(payload, (("cell", 1),), OBS_CAP)
    own_anom = window[:mem_dev].astype(jnp.bfloat16)
    own_innov = window[mem_dev : 2 * mem_dev].astype(jnp.bfloat16)
    all_anom, all_innov = side_by_side((own_anom, own_innov), "mem", 0, 1)
    win_anom = three_tiles(all_anom, tiles)
    win_innov = three_tiles(all_innov, tiles)
    win_pos = three_tiles(window[2 * mem_dev], tiles)
    groups = lax.axis_size("mem")
    member_group = lax.axis_index("mem")
    piece = C_TILE // groups
    arranged = jnp.transpose(state.reshape(mem_dev, tiles, groups, piece), (0, 2, 1, 3)).reshape(
        mem_dev, groups, tiles * piece
    )
    split_state = lax.all_to_all(arranged, "mem", split_axis=1, concat_axis=0, tiled=True)
    split_f32 = split_state.reshape(MEMBERS, tiles, piece).astype(jnp.float32)
    mean_share = lax.dynamic_index_in_dim(
        ens_mean.reshape(tiles, groups, piece), member_group, 1, keepdims=False
    )
    split_anom = (split_f32 - mean_share[None]).astype(jnp.bfloat16)
    covariance = jnp.einsum(
        "mtc,mto->tco", split_anom, win_anom, preferred_element_type=jnp.float32
    ) / (MEMBERS - 1)
    cell_pos = (
        base
        + lax.iota(jnp.int32, tiles)[:, None] * C_TILE
        + member_group * piece
        + lax.iota(jnp.int32, piece)[None, :]
    ).astype(jnp.float32)
    gain_mat = tapered(cell_pos, win_pos, covariance)
    increment = jnp.einsum("mto,tco->mtc", win_innov, gain_mat, preferred_element_type=jnp.float32)
    split_out = (split_f32 + increment).astype(jnp.bfloat16).reshape(MEMBERS, 1, tiles * piece)
    returned = lax.all_to_all(split_out, "mem", split_axis=0, concat_axis=1, tiled=True)
    return jnp.transpose(returned.reshape(mem_dev, groups, tiles, piece), (0, 2, 1, 3)).reshape(
        mem_dev, cell_count
    )


def solution(mesh):
    placed = (
        P("mem", "cell"),
        P("cell"),
        P("cell"),
        P("cell"),
        P("cell"),
        P("cell"),
        P("mem", None),
    )
    return jax.shard_map(
        body, mesh=mesh, in_specs=placed, out_specs=P("mem", "cell"), check_vma=False
    )
```

profile of v0, /device:TPU:70, one launch (start us, length us, event | category | flops | bytes accessed | tf_op | source)
XLA Modules:
  0.0 250.0 jit_solution(8026473560259197599)
XLA Ops:
  6.5 5.0 %copy.97 = f32[8,16384]{0,1:T(8,128)} copy(bf16[8,16384]{1,0:T(8,128)(2,1)} %param.7) | data formatting | bytes 786432 | tf_op jit(solution)/shard_map/convert_element_type | solution.py:80
  11.5 0.2 convert_reduce_fusion
  11.7 8.8 %gather_fusion = f32[2048,8]{1,0:T(8,128)S(1)} fusion(f32[8,16384]{0,1:T(8,128)} %copy.97, s32[2048]{0:T(1024)S(1)} %get-tuple-element.21), kind=kCustom, calls=%fused_computation | custom fusion | bytes 139264 | tf_op jit(solution)/shard_map/jit(_take)/gather | solution.py:81
  20.6 0.3 copy.98
  20.9 1.6 broadcast_in_dim.56
  22.6 18.4 %all-to-all-start.1 = ((f32[16,1,18432]{2,1,0:T(1,128)}), f32[16,1,18432]{2,1,0:T(1,128)S(1)}, u32[]{:S(2)}, u32[]{:S(2)}) async-start(f32[16,1,18432]{2,1,0:T(1,128)} %broadcast_in_dim.56), calls=%async_computation.1 | async-start | bytes 2359296 | tf_op jit(solution)/shard_map/all_to_all | solution.py:15
  41.1 55.1 %all-to-all-done.1 = f32[16,1,18432]{2,1,0:T(1,128)S(1)} async-done(((f32[16,1,18432]{2,1,0:T(1,128)}), f32[16,1,18432]{2,1,0:T(1,128)S(1)}, u32[]{:S(2)}, u32[]{:S(2)}) %all-to-all-start.1) | async-done | bytes 1179680 | tf_op jit(solution)/shard_map/all_to_all | solution.py:15
  96.2 0.7 reduce_sum.29
  97.0 11.8 %gather_fusion.2 = f32[2048]{0:T(1024)S(1)} fusion(f32[16384]{0:T(1024)S(1)} %slice_multiply_fusion, s32[2048]{0:T(1024)S(1)} %get-tuple-element.21), kind=kCustom, calls=%fused_computation.2 | custom fusion | bytes 24576 | tf_op jit(solution)/shard_map/jit(_take)/gather | solution.py:90
  108.9 3.4 %copy.100 = bf16[8,16384]{0,1:T(8,128)(2,1)} copy(bf16[8,16384]{1,0:T(8,128)(2,1)S(1)} %subtract_convert_fusion.1) | data formatting | bytes 524288 | tf_op jit(solution)/shard_map/convert_element_type | solution.py:88
  112.3 8.3 %gather_fusion.1 = bf16[2048,8]{1,0:T(8,128)(2,1)S(1)} fusion(bf16[8,16384]{0,1:T(8,128)(2,1)} %copy.100, s32[2048]{0:T(1024)S(1)} %get-tuple-element.21), kind=kCustom, calls=%fused_computation.1 | custom fusion | bytes 73728 | tf_op jit(solution)/shard_map/jit(_take)/gather | solution.py:89
  120.6 0.2 copy.101
  120.9 1.4 fusion.8
  122.3 1.9 collective-permute-start
  124.2 3.6 %collective-permute-start.1 = (f32[17,128]{1,0:T(8,128)S(1)}, f32[17,128]{1,0:T(8,128)S(1)}, u32[]{:S(2)}, u32[]{:S(2)}) collective-permute-start(f32[17,128]{1,0:T(8,128)S(1)} %get-tuple-element.18), channel_id=1, source_target_pairs={{16,0},{32,16},{48,32},{64,48},{80,64},{96,80},{112,96},{128,112},... | collective-permute-start | bytes 26120 | tf_op jit(solution)/shard_map/ppermute | solution.py:39
  127.9 1.4 collective-permute-done.1
  129.3 0.6 pad_maximum_fusion.5
  129.9 0.5 reshape.120
  130.5 0.1 copy.96
  130.6 1.1 reshape.121
  131.7 8.2 %all-to-all-start = ((bf16[8,16,1024]{2,0,1:T(8,128)(2,1)}), bf16[8,16,1024]{2,0,1:T(8,128)(2,1)S(1)}, u32[]{:S(2)}, u32[]{:S(2)}) async-start(bf16[8,16,1024]{2,0,1:T(8,128)(2,1)} %reshape.121), calls=%async_computation | async-start | bytes 524288 | tf_op jit(solution)/shard_map/all_to_all | solution.py:113
  140.0 17.7 %all-to-all-done = bf16[8,16,1024]{2,0,1:T(8,128)(2,1)S(1)} async-done(((bf16[8,16,1024]{2,0,1:T(8,128)(2,1)}), bf16[8,16,1024]{2,0,1:T(8,128)(2,1)S(1)}, u32[]{:S(2)}, u32[]{:S(2)}) %all-to-all-start) | async-done | bytes 262176 | tf_op jit(solution)/shard_map/all_to_all | solution.py:113
  157.8 0.3 reshape.127
  158.0 0.4 copy.111
  158.6 0.9 subtract_convert_fusion
  159.5 45.9 %all-gather.2.cloned.1.call-done = bf16[128,4608]{1,0:T(8,128)(2,1)} async-done(((bf16[8,4608]{1,0:T(8,128)(2,1)}), bf16[128,4608]{1,0:T(8,128)(2,1)}) %all-gather.2.cloned.1.call-update) | async-done | bytes 1179664 | tf_op jit(solution)/shard_map/all_gather | solution.py:46
  205.3 1.3 fusion.56
  206.7 0.3 copy.102
  207.0 0.4 fusion.57
  207.3 1.0 copy.119
  208.4 1.0 copy.120
  209.4 1.0 copy.121
  210.4 0.3 copy.107
  210.7 0.4 fusion.58
  211.1 1.0 copy.122
  212.1 1.0 copy.123
  213.1 0.3 copy.124
  213.4 2.8 %fusion.31 = bf16[128,16,64]{0,2,1:T(8,128)(2,1)S(1)} fusion(f32[128,16,64]{0,2,1:T(8,128)S(1)} %copy.111, bf16[128,16,128]{2,0,1:T(8,128)(2,1)S(1)} %copy.124, bf16[128,16,128]{2,0,1:T(8,128)(2,1)} %copy.123, bf16[128,16,128]{2,0,1:T(8,128)(2,1)} %copy.122, bf16[128,16,128]{2,0,1:T(8,128)(2,1)} %copy.121, bf16[128,16,128]{2,0,1:T(8,128)(2,1)S(1)} %copy-done.4, ...), kind=kOutput, calls=%fused_computation.31 | convolution fusion | flops 215351296 | bytes 4222976 | tf_op jit(solution)/shard_map/mto,tco->mtc/dot_general | solution.py:129
  216.3 0.5 broadcast.101
  216.8 0.8 reduce.2
  217.6 0.1 copy.130
  217.8 0.2 reshape.157
  217.9 23.0 %all_to_all.30 = bf16[16,2,4096]{2,1,0:T(2,128)(2,1)S(1)} all-to-all(bf16[16,2,4096]{2,1,0:T(2,128)(2,1)S(1)} %reshape.157), channel_id=1, replica_groups=mesh['cell'=64,'mem'=16] {'mem'}, dimensions={0} | all-to-all | bytes 524288 | tf_op jit(solution)/shard_map/all_to_all | solution.py:131
  240.9 0.3 reshape.158
  241.3 0.2 copy.113
  241.5 0.3 reshape.125
  241.8 0.1 copy.114
  242.0 1.2 reshape.126
  (42 shorter events, 0.7 us)
Async XLA Ops:
  6.5 114.3 %copy-start = (f32[8,512]{1,0:T(8,128)S(1)}, f32[8,512]{1,0:T(8,128)}, u32[]{:S(2)}) copy-start(f32[8,512]{1,0:T(8,128)} %param.13) | copy-start | bytes 49156
  6.5 5.0 %copy-start.1 = (bf16[8,16384]{1,0:T(8,128)(2,1)S(1)}, bf16[8,16384]{1,0:T(8,128)(2,1)}, u32[]{:S(2)}) copy-start(bf16[8,16384]{1,0:T(8,128)(2,1)} %param.7) | copy-start | bytes 786436
  6.5 5.1 %copy-start.5 = (s32[2048]{0:T(1024)S(1)}, s32[2048]{0:T(1024)}, u32[]{:S(2)}) copy-start(s32[2048]{0:T(1024)} %param.10) | copy-start | bytes 24580
  20.9 20.1 %copy-start.7 = (s32[16]{0:T(128)S(1)}, s32[16]{0:T(128)}, u32[]{:S(2)}) copy-start(s32[16]{0:T(128)} %param.11) | copy-start | bytes 196
  22.6 73.7 %all-to-all-start.1 = ((f32[16,1,18432]{2,1,0:T(1,128)}), f32[16,1,18432]{2,1,0:T(1,128)S(1)}, u32[]{:S(2)}, u32[]{:S(2)}) async-start(f32[16,1,18432]{2,1,0:T(1,128)} %broadcast_in_dim.56), calls=%async_computation.1 | async-start | bytes 2359296 | tf_op jit(solution)/shard_map/all_to_all | solution.py:15
  41.0 164.3 %all-gather.2.cloned.1.call-start = ((), (), s32[]{:S(2)}) async-start(), calls=%async_computation.3 | async-start | bytes 1253376 | tf_op jit(solution)/shard_map/all_gather | solution.py:46
  108.8 12.0 %copy-start.6 = (f32[2048]{0:T(1024)S(1)}, f32[2048]{0:T(1024)}, u32[]{:S(2)}) copy-start(f32[2048]{0:T(1024)} %param.9) | copy-start | bytes 24580
  108.9 12.0 %copy-start.8 = (s32[2048]{0:T(1024)S(1)}, s32[2048]{0:T(1024)}, u32[]{:S(2)}) copy-start(s32[2048]{0:T(1024)} %param.12) | copy-start | bytes 24580
  108.9 12.0 %copy-start.9 = (f32[2048]{0:T(1024)S(1)}, f32[2048]{0:T(1024)}, u32[]{:S(2)}) copy-start(f32[2048]{0:T(1024)} %param.8) | copy-start | bytes 24580
  122.3 5.6 %collective-permute-start = (f32[17,128]{1,0:T(8,128)S(1)}, f32[17,128]{1,0:T(8,128)S(1)}, u32[]{:S(2)}, u32[]{:S(2)}) collective-permute-start(f32[17,128]{1,0:T(8,128)S(1)} %get-tuple-element.17), channel_id=1, source_target_pairs={{0,16},{16,32},{32,48},{48,64},{64,80},{80,96},{96,112},{112,128},... | collective-permute-start | bytes 26120 | tf_op jit(solution)/shard_map/ppermute | solution.py:36
  124.2 5.0 %collective-permute-start.1 = (f32[17,128]{1,0:T(8,128)S(1)}, f32[17,128]{1,0:T(8,128)S(1)}, u32[]{:S(2)}, u32[]{:S(2)}) collective-permute-start(f32[17,128]{1,0:T(8,128)S(1)} %get-tuple-element.18), channel_id=1, source_target_pairs={{16,0},{32,16},{48,32},{64,48},{80,64},{96,80},{112,96},{128,112},... | collective-permute-start | bytes 26120 | tf_op jit(solution)/shard_map/ppermute | solution.py:39
  131.7 26.0 %all-to-all-start = ((bf16[8,16,1024]{2,0,1:T(8,128)(2,1)}), bf16[8,16,1024]{2,0,1:T(8,128)(2,1)S(1)}, u32[]{:S(2)}, u32[]{:S(2)}) async-start(bf16[8,16,1024]{2,0,1:T(8,128)(2,1)} %reshape.121), calls=%async_computation | async-start | bytes 524288 | tf_op jit(solution)/shard_map/all_to_all | solution.py:113
  211.1 2.3 copy-start.2
  211.1 2.3 copy-start.3
  212.1 1.3 copy-start.4
Sparse Core Ops, SparseCore 0:
  130.0 75.2 all-gather.1
where the time goes:
time: 250 us
  waiting for transfers between devices  120 us (48%)
  local copies, waits for them, and re-layouts  53 us (21%)
  starting transfers between devices  32.3 us (13%)
  blocking collectives  23 us (9%)
  between operations  13.8 us (6%)
  matrix products  4.22 us (2%)
  other arithmetic  3.61 us (1%)
    all_to_all x1, waiting for transfers between devices, copy_for_each(): lax.all_to_all(jnp.broadcast_to(x[None], (devices, *x.shape)), axis, 0, 0...  55.1 us
    all_gather x1, waiting for transfers between devices, side_by_side(): lax.all_gather(both, axis, axis=dim, tiled=True)  45.9 us
    all_to_all x1, blocking collectives, body(): lax.all_to_all(split_out, 'mem', split_axis=0, concat_axis=1, tiled=True)  23 us
    all_to_all x1, starting transfers between devices, copy_for_each(): lax.all_to_all(jnp.broadcast_to(x[None], (devices, *x.shape)), axis, 0, 0...  18.4 us
    all_to_all x1, waiting for transfers between devices, body(): lax.all_to_all(arranged, 'mem', split_axis=1, concat_axis=0, tiled=True)  17.7 us
    gather x1, local copies, waits for them, and re-layouts, body(): mean_at = jnp.take(ens_mean, local_cell)  11.8 us
    gather x2, local copies, waits for them, and re-layouts, body(): at_obs = jnp.take(state_f32, local_cell, axis=1)  9.14 us
    gather x2, local copies, waits for them, and re-layouts, body(): jnp.take(anomaly, local_cell, axis=1) * live_mask.astype(jnp.bfloat16)  8.5 us
  transfers between devices with their start and end apart: 5, of which 4 were waited for; matrix products, arithmetic and copies ran while one was open for 1% of the time, Pallas kernels for 0%

commit v1 on v0

v1 whole, which is shorter than its diff:
```python
import jax
import jax.numpy as jnp
from jax import lax
from jax.experimental import pallas as pl
from jax.experimental.pallas import tpu as pltpu
from jax.sharding import PartitionSpec as P

MEMBERS = 128
C_TILE = 1024
OBS_CAP = 128
NOISE = 512
LOCALIZE = 1024
LANES = 128
CHUNK = 256
POS_BASE = 32
F32 = jnp.float32
BF16 = jnp.bfloat16


def pack_kernel(state_ref, noise_ref, pick_ref, out_ref):
    tiles = out_ref.shape[0]
    mem_dev = state_ref.shape[0]
    table = [noise_ref[:, k * LANES : (k + 1) * LANES] for k in range(NOISE // LANES)]
    for t in range(tiles):
        out_ref[t, :, 0:C_TILE] = state_ref[:, t * C_TILE : (t + 1) * C_TILE]
        pick = jnp.broadcast_to(pick_ref[t : t + 1, :], (mem_dev, OBS_CAP))
        lane, block = pick % LANES, pick // LANES
        chosen = jnp.zeros((mem_dev, OBS_CAP), F32)
        for k, part in enumerate(table):
            here = jnp.take_along_axis(part, lane, axis=1)
            chosen = jnp.where(block == k, here, chosen)
        out_ref[t, :, C_TILE : C_TILE + OBS_CAP] = chosen.astype(BF16)


def pack(state, noise_table, picks):
    mem_dev = state.shape[0]
    tiles = picks.shape[0]
    return pl.pallas_call(
        pack_kernel,
        out_shape=jax.ShapeDtypeStruct((tiles, mem_dev, C_TILE + OBS_CAP), BF16),
        name="pack",
    )(state, noise_table, picks)


def obs_kernel(which_ref, count_ref, tile_ref, value_ref, error_ref, cell_ref, send_ref, anom_ref):
    me = which_ref[0]
    value = value_ref[pl.ds(me, 1), :]
    error = error_ref[pl.ds(me, 1), :]
    cell = cell_ref[pl.ds(me, 1), :]
    live = (lax.broadcasted_iota(jnp.int32, (1, OBS_CAP), 1) < count_ref[me]).astype(F32)
    state = tile_ref[:, 0:C_TILE]
    onehot = (lax.broadcasted_iota(jnp.int32, (C_TILE, OBS_CAP), 0) == cell).astype(F32).astype(BF16)
    at_obs = jnp.dot(state, onehot, preferred_element_type=F32)
    perturb = tile_ref[:, C_TILE : C_TILE + OBS_CAP].astype(F32)
    mean_at = jnp.sum(at_obs, axis=0, keepdims=True) / MEMBERS
    spread = (jnp.sum(at_obs * at_obs, axis=0, keepdims=True) - MEMBERS * mean_at * mean_at) / (
        MEMBERS - 1
    )
    weight = live / (spread + error)
    innovation = (value + jnp.sqrt(error) * perturb - at_obs) * weight
    send_ref[0:MEMBERS, :] = ((at_obs - mean_at) * live).astype(BF16)
    send_ref[MEMBERS : 2 * MEMBERS, :] = innovation.astype(BF16)
    row = lax.broadcasted_iota(jnp.int32, (16, OBS_CAP), 0)
    digits = jnp.where(row == 0, cell // POS_BASE, cell % POS_BASE)
    send_ref[2 * MEMBERS : 2 * MEMBERS + 16, :] = digits.astype(F32).astype(BF16)
    state_f32 = state.astype(F32)
    mean = jnp.sum(state_f32, axis=0, keepdims=True) / MEMBERS
    anom_ref[...] = (state_f32 - mean).astype(BF16)


def obs_stage(which, counts, tile, value, error, cell):
    smem = pl.BlockSpec(memory_space=pltpu.SMEM)
    vmem = pl.BlockSpec(memory_space=pltpu.VMEM)
    return pl.pallas_call(
        obs_kernel,
        in_specs=[smem, smem, vmem, vmem, vmem, vmem],
        out_shape=(
            jax.ShapeDtypeStruct((2 * MEMBERS + 16, OBS_CAP), BF16),
            jax.ShapeDtypeStruct((MEMBERS, C_TILE), BF16),
        ),
        name="obs",
    )(which, counts, tile, value, error, cell)


def increment_of(anom, sent_ref, shift):
    digits = sent_ref[2 * MEMBERS : 2 * MEMBERS + 16, :].astype(F32)
    position = digits[0:1, :] * POS_BASE + digits[1:2, :] + shift
    position = jnp.transpose(jnp.broadcast_to(position, (OBS_CAP, OBS_CAP)))
    covariance = lax.dot_general(
        sent_ref[0:MEMBERS, :], anom, (((0,), (0,)), ((), ())), preferred_element_type=F32
    )
    width = anom.shape[1]
    away = lax.broadcasted_iota(jnp.int32, (OBS_CAP, width), 1).astype(F32) - jnp.concatenate(
        [position] * (width // OBS_CAP), axis=1
    )
    inner = jnp.maximum(1.0 - (away * away) * (1.0 / (LOCALIZE * LOCALIZE)), 0.0)
    gain = (inner * inner * (covariance * (1.0 / (MEMBERS - 1)))).astype(BF16)
    return jnp.dot(sent_ref[MEMBERS : 2 * MEMBERS, :], gain, preferred_element_type=F32)


def own_kernel(tile_ref, anom_ref, sent_ref, out_ref):
    for start in range(0, C_TILE, CHUNK):
        cut = slice(start, start + CHUNK)
        part = increment_of(anom_ref[:, cut], sent_ref, -start)
        out_ref[:, cut] = tile_ref[:, cut].astype(F32) + part


def side_kernel(so_far_ref, anom_ref, low_ref, high_ref, out_ref):
    for start in range(0, C_TILE, CHUNK):
        cut = slice(start, start + CHUNK)
        anom = anom_ref[:, cut]
        total = so_far_ref[:, cut]
        total = total + increment_of(anom, low_ref, -C_TILE - start)
        total = total + increment_of(anom, high_ref, C_TILE - start)
        out_ref[:, cut] = total.astype(BF16)


def body(state, obs_value, obs_error, obs_cell, obs_count, obs_noise, noise_table):
    mem_dev, cell_count = state.shape
    tiles = cell_count // C_TILE
    rows = lambda a: a.reshape(tiles, OBS_CAP)
    packed = pack(state, noise_table, rows(obs_noise))
    tile = lax.all_to_all(packed, "mem", split_axis=0, concat_axis=0, tiled=True)
    tile = tile.reshape(MEMBERS, C_TILE + OBS_CAP)
    which = lax.axis_index("mem").reshape(1)
    sent, anom = obs_stage(which, obs_count, tile, rows(obs_value), rows(obs_error), rows(obs_cell))
    both = ("cell", "mem")
    total = lax.axis_size("cell") * lax.axis_size("mem")
    low = lax.ppermute(sent, both, [(i, i + 1) for i in range(total - 1)])
    high = lax.ppermute(sent, both, [(i + 1, i) for i in range(total - 1)])
    so_far = pl.pallas_call(
        own_kernel, out_shape=jax.ShapeDtypeStruct((MEMBERS, C_TILE), F32), name="own"
    )(tile, anom, sent)
    analysis = pl.pallas_call(
        side_kernel, out_shape=jax.ShapeDtypeStruct((MEMBERS, C_TILE), BF16), name="side"
    )(so_far, anom, low, high)
    returned = lax.all_to_all(
        analysis.reshape(tiles, mem_dev, C_TILE), "mem", split_axis=0, concat_axis=0, tiled=True
    )
    return jnp.transpose(returned, (1, 0, 2)).reshape(mem_dev, cell_count)


def solution(mesh):
    placed = (
        P("mem", "cell"),
        P("cell"),
        P("cell"),
        P("cell"),
        P("cell"),
        P("cell"),
        P("mem", None),
    )
    return jax.shard_map(
        body, mesh=mesh, in_specs=placed, out_specs=P("mem", "cell"), check_vma=False
    )
```

time: 250 us -> 83.8 us (0.34)
  the two profiles are of different devices: /device:TPU:70 before, /device:TPU:31 now
where the time goes in v1:
time: 83.8 us; the launch traced here: 83.4 us
  starting transfers between devices  32.5 us (39%)
  blocking collectives  25.5 us (30%)
  waiting for transfers between devices  14.2 us (17%)
  Pallas kernels  8.49 us (10%)
  local copies, waits for them, and re-layouts  2.67 us (3%)
    all_to_all x1, blocking collectives, body(): lax.all_to_all(analysis.reshape(tiles, mem_dev, C_TILE), 'mem', split_axi...  25.5 us
    all_to_all x1, starting transfers between devices, body(): lax.all_to_all(packed, 'mem', split_axis=0, concat_axis=0, tiled=True)  18.6 us
    all_to_all x1, waiting for transfers between devices, body(): lax.all_to_all(packed, 'mem', split_axis=0, concat_axis=0, tiled=True)  14.2 us
    ppermute x1, starting transfers between devices, body(): low = lax.ppermute(sent, both, [(i, i + 1) for i in range(total - 1)])  7.78 us
    ppermute x1, starting transfers between devices, body(): high = lax.ppermute(sent, both, [(i + 1, i) for i in range(total - 1)])  6.15 us
    unnamed x7, local copies, waits for them, and re-layouts  2.67 us
    pallas_call x1, Pallas kernels, body(): pl.pallas_call(side_kernel, out_shape=jax.ShapeDtypeStruct((MEMBERS, C_TI...  2.44 us
    pallas_call x1, Pallas kernels, body(): pl.pallas_call(own_kernel, out_shape=jax.ShapeDtypeStruct((MEMBERS, C_TIL...  2.3 us
  transfers between devices with their start and end apart: 3, of which 1 were waited for; matrix products, arithmetic and copies ran while one was open for 0% of the time, Pallas kernels for 3%

profile of v1, /device:TPU:31, one launch (start us, length us, event | category | flops | bytes accessed | tf_op | source)
XLA Modules:
  0.0 83.4 jit_solution(12345351007708390213)
XLA Ops:
  0.0 1.8 %pack.1 = bf16[16,8,1152]{2,1,0:T(8,128)(2,1)} custom-call(bf16[8,16384]{1,0:T(8,128)(2,1)} %state_ref.1, f32[8,512]{1,0:T(8,128)} %noise_ref.1, s32[16,128]{1,0:T(8,128)} %bitcast.14), custom_call_target="tpu_custom_call" | custom-call | tf_op jit(solution)/shard_map/pack/pallas_call | solution.py:38
  1.8 18.6 %all-to-all-start = ((bf16[16,8,1152]{2,1,0:T(8,128)(2,1)}), bf16[16,8,1152]{2,1,0:T(8,128)(2,1)S(1)}, u32[]{:S(2)}, u32[]{:S(2)}) async-start(bf16[16,8,1152]{2,1,0:T(8,128)(2,1)} %pack.1), calls=%async_computation | async-start | bytes 589824 | tf_op jit(solution)/shard_map/all_to_all | solution.py:123
  20.4 14.2 %all-to-all-done = bf16[16,8,1152]{2,1,0:T(8,128)(2,1)S(1)} async-done(((bf16[16,8,1152]{2,1,0:T(8,128)(2,1)}), bf16[16,8,1152]{2,1,0:T(8,128)(2,1)S(1)}, u32[]{:S(2)}, u32[]{:S(2)}) %all-to-all-start) | async-done | bytes 294944 | tf_op jit(solution)/shard_map/all_to_all | solution.py:123
  34.6 0.0 copy-start
  34.6 0.7 copy-done
  35.3 1.9 %obs.1 = (bf16[272,128]{1,0:T(8,128)(2,1)}, bf16[128,1024]{1,0:T(8,128)(2,1)}) custom-call(s32[1]{0:T(128)} %bitcast.2.which_ref, s32[16]{0:T(128)} %count_ref.1, bf16[128,1152]{1,0:T(8,128)(2,1)} %bitcast.10, f32[16,128]{1,0:T(8,128)} %bitcast.15, f32[16,128]{1,0:T(8,128)} %bitcast.16, s32[16,128]{1,0:T(8,128)} %bitcast.17), custom_call_target="tpu_custom_call" | custom-call | tf_op jit(solution)/shard_map/obs/pallas_call | solution.py:74
  37.2 7.8 %collective-permute-start = (bf16[272,128]{1,0:T(8,128)(2,1)}, bf16[272,128]{1,0:T(8,128)(2,1)S(1)}, u32[]{:S(2)}, u32[]{:S(2)}) collective-permute-start(bf16[272,128]{1,0:T(8,128)(2,1)} %get-tuple-element.8.sent_ref), channel_id=1, source_target_pairs={{0,1},{1,2},{2,3},{3,4},{4,5},{5,6},{6,7},{7,8},{8,9},{9,10},{10,1... | collective-permute-start | bytes 208904 | tf_op jit(solution)/shard_map/ppermute | solution.py:129
  45.0 6.2 %collective-permute-start.1 = (bf16[272,128]{1,0:T(8,128)(2,1)}, bf16[272,128]{1,0:T(8,128)(2,1)S(1)}, u32[]{:S(2)}, u32[]{:S(2)}) collective-permute-start(bf16[272,128]{1,0:T(8,128)(2,1)} %get-tuple-element.8.sent_ref), channel_id=1, source_target_pairs={{1,0},{2,1},{3,2},{4,3},{5,4},{6,5},{7,6},{8,7},{9,8},{10,9},{11,1... | collective-permute-start | bytes 208904 | tf_op jit(solution)/shard_map/ppermute | solution.py:130
  51.2 2.3 %own.1.so_far_ref = f32[128,1024]{1,0:T(8,128)} custom-call(bf16[128,1152]{1,0:T(8,128)(2,1)} %bitcast.11, bf16[128,1024]{1,0:T(8,128)(2,1)} %get-tuple-element.7.anom_ref, bf16[272,128]{1,0:T(8,128)(2,1)} %get-tuple-element.8.sent_ref), custom_call_target="tpu_custom_call" | custom-call | tf_op jit(solution)/shard_map/own/pallas_call | solution.py:131
  53.5 0.0 collective-permute-done.low_ref
  53.5 0.0 copy-start.1
  53.5 0.0 collective-permute-done.1.high_ref
  53.5 0.6 copy-done.1
  54.1 0.0 copy-start.2
  54.1 0.6 copy-done.2
  54.7 2.4 %side.1 = bf16[128,1024]{1,0:T(8,128)(2,1)} custom-call(f32[128,1024]{1,0:T(8,128)} %own.1.so_far_ref, bf16[128,1024]{1,0:T(8,128)(2,1)} %get-tuple-element.7.anom_ref, bf16[272,128]{1,0:T(8,128)(2,1)} %copy-done.1, bf16[272,128]{1,0:T(8,128)(2,1)} %copy-done.2), custom_call_target="tpu_custom_call" | custom-call | tf_op jit(solution)/shard_map/side/pallas_call | solution.py:134
  57.2 25.5 %all_to_all.10 = bf16[16,8,1024]{2,1,0:T(8,128)(2,1)S(1)} all-to-all(bf16[16,8,1024]{2,1,0:T(8,128)(2,1)} %bitcast.13), channel_id=1, replica_groups=mesh['cell'=64,'mem'=16] {'mem'}, dimensions={0} | all-to-all | bytes 524288 | tf_op jit(solution)/shard_map/all_to_all | solution.py:137
  82.7 0.7 copy.9
Async XLA Ops:
  1.8 32.8 %all-to-all-start = ((bf16[16,8,1152]{2,1,0:T(8,128)(2,1)}), bf16[16,8,1152]{2,1,0:T(8,128)(2,1)S(1)}, u32[]{:S(2)}, u32[]{:S(2)}) async-start(bf16[16,8,1152]{2,1,0:T(8,128)(2,1)} %pack.1), calls=%async_computation | async-start | bytes 589824 | tf_op jit(solution)/shard_map/all_to_all | solution.py:123
  34.6 0.7 copy-start
  37.2 16.2 %collective-permute-start = (bf16[272,128]{1,0:T(8,128)(2,1)}, bf16[272,128]{1,0:T(8,128)(2,1)S(1)}, u32[]{:S(2)}, u32[]{:S(2)}) collective-permute-start(bf16[272,128]{1,0:T(8,128)(2,1)} %get-tuple-element.8.sent_ref), channel_id=1, source_target_pairs={{0,1},{1,2},{2,3},{3,4},{4,5},{5,6},{6,7},{7,8},{8,9},{9,10},{10,1... | collective-permute-start | bytes 208904 | tf_op jit(solution)/shard_map/ppermute | solution.py:129
  45.0 8.5 %collective-permute-start.1 = (bf16[272,128]{1,0:T(8,128)(2,1)}, bf16[272,128]{1,0:T(8,128)(2,1)S(1)}, u32[]{:S(2)}, u32[]{:S(2)}) collective-permute-start(bf16[272,128]{1,0:T(8,128)(2,1)} %get-tuple-element.8.sent_ref), channel_id=1, source_target_pairs={{1,0},{2,1},{3,2},{4,3},{5,4},{6,5},{7,6},{8,7},{9,8},{10,9},{11,1... | collective-permute-start | bytes 208904 | tf_op jit(solution)/shard_map/ppermute | solution.py:130
  53.5 0.6 copy-start.1
  54.1 0.6 copy-start.2

commit v2 on v1

--- a/solution.py
+++ b/solution.py
@@ -37,7 +37,7 @@
     tiles = picks.shape[0]
     return pl.pallas_call(
         pack_kernel,
-        out_shape=jax.ShapeDtypeStruct((tiles, mem_dev, C_TILE + OBS_CAP), BF16),
+        out_shape=pltpu.VMEM((tiles, mem_dev, C_TILE + OBS_CAP), BF16),
         name="pack",
     )(state, noise_table, picks)
 
@@ -71,12 +71,13 @@
 def obs_stage(which, counts, tile, value, error, cell):
     smem = pl.BlockSpec(memory_space=pltpu.SMEM)
     vmem = pl.BlockSpec(memory_space=pltpu.VMEM)
+    tile = pltpu.with_memory_space_constraint(tile, pltpu.VMEM)
     return pl.pallas_call(
         obs_kernel,
         in_specs=[smem, smem, vmem, vmem, vmem, vmem],
         out_shape=(
-            jax.ShapeDtypeStruct((2 * MEMBERS + 16, OBS_CAP), BF16),
-            jax.ShapeDtypeStruct((MEMBERS, C_TILE), BF16),
+            pltpu.VMEM((2 * MEMBERS + 16, OBS_CAP), BF16),
+            pltpu.VMEM((MEMBERS, C_TILE), BF16),
         ),
         name="obs",
     )(which, counts, tile, value, error, cell)
@@ -128,12 +129,13 @@
     total = lax.axis_size("cell") * lax.axis_size("mem")
     low = lax.ppermute(sent, both, [(i, i + 1) for i in range(total - 1)])
     high = lax.ppermute(sent, both, [(i + 1, i) for i in range(total - 1)])
+    v = lambda a: pltpu.with_memory_space_constraint(a, pltpu.VMEM)
     so_far = pl.pallas_call(
-        own_kernel, out_shape=jax.ShapeDtypeStruct((MEMBERS, C_TILE), F32), name="own"
-    )(tile, anom, sent)
+        own_kernel, out_shape=pltpu.VMEM((MEMBERS, C_TILE), F32), name="own"
+    )(v(tile), v(anom), v(sent))
     analysis = pl.pallas_call(
-        side_kernel, out_shape=jax.ShapeDtypeStruct((MEMBERS, C_TILE), BF16), name="side"
-    )(so_far, anom, low, high)
+        side_kernel, out_shape=pltpu.VMEM((MEMBERS, C_TILE), BF16), name="side"
+    )(v(so_far), v(anom), v(low), v(high))
     returned = lax.all_to_all(
         analysis.reshape(tiles, mem_dev, C_TILE), "mem", split_axis=0, concat_axis=0, tiled=True
     )

time: 83.8 us -> 79.3 us (0.946)
  Pallas kernels: 8.49 us -> 3.97 us
  local copies, waits for them, and re-layouts: 2.67 us -> 0.7 us
  waiting for transfers between devices: 14.2 us -> 15.6 us
    pallas_call x3, Pallas kernels: 6.59 us -> 2.88 us  [the longest x1 1.83 us: pack(): pl.pallas_call(pack_kernel, out_shape=pltpu.VMEM((tiles, mem_dev, C_TILE...]
    unnamed x7 -> x1, local copies, waits for them, and re-layouts: 2.67 us -> 0.7 us
    ppermute x1, waiting for transfers between devices: 0.01 us -> 1.42 us  [body(): high = lax.ppermute(sent, both, [(i + 1, i) for i in range(total - 1)])]
  transfers between devices with their start and end apart: 3 -> 3, of which waited for: 1 -> 2; matrix products, arithmetic and copies ran while one was open for 0% -> 0% of each run, Pallas kernels for 3% -> 1%
where the time goes in v2:
time: 79.3 us; the launch traced here: 79 us
  starting transfers between devices  32.5 us (41%)
  blocking collectives  26.1 us (33%)
  waiting for transfers between devices  15.6 us (20%)
  Pallas kernels  3.97 us (5%)
    all_to_all x1, blocking collectives, body(): lax.all_to_all(analysis.reshape(tiles, mem_dev, C_TILE), 'mem', split_axi...  26.1 us
    all_to_all x1, starting transfers between devices, body(): lax.all_to_all(packed, 'mem', split_axis=0, concat_axis=0, tiled=True)  18.6 us
    all_to_all x1, waiting for transfers between devices, body(): lax.all_to_all(packed, 'mem', split_axis=0, concat_axis=0, tiled=True)  14.2 us
    ppermute x1, starting transfers between devices, body(): low = lax.ppermute(sent, both, [(i, i + 1) for i in range(total - 1)])  7.79 us
    ppermute x1, starting transfers between devices, body(): high = lax.ppermute(sent, both, [(i + 1, i) for i in range(total - 1)])  6.15 us
    pallas_call x1, Pallas kernels, pack(): pl.pallas_call(pack_kernel, out_shape=pltpu.VMEM((tiles, mem_dev, C_TILE...  1.83 us
  transfers between devices with their start and end apart: 3, of which 2 were waited for; matrix products, arithmetic and copies ran while one was open for 0% of the time, Pallas kernels for 1%

profile of v2, /device:TPU:31, one launch (start us, length us, event | category | flops | bytes accessed | tf_op | source)
XLA Modules:
  0.0 79.0 jit_solution(11117078157958397247)
XLA Ops:
  0.0 1.8 %pack.1 = bf16[16,8,1152]{2,1,0:T(8,128)(2,1)} custom-call(bf16[8,16384]{1,0:T(8,128)(2,1)} %state_ref.1, f32[8,512]{1,0:T(8,128)} %noise_ref.1, s32[16,128]{1,0:T(8,128)} %bitcast.14), custom_call_target="tpu_custom_call" | custom-call | tf_op jit(solution)/shard_map/pack/pallas_call | solution.py:38
  1.8 18.6 %all-to-all-start = ((bf16[16,8,1152]{2,1,0:T(8,128)(2,1)}), bf16[16,8,1152]{2,1,0:T(8,128)(2,1)S(1)}, u32[]{:S(2)}, u32[]{:S(2)}) async-start(bf16[16,8,1152]{2,1,0:T(8,128)(2,1)} %pack.1), calls=%async_computation | async-start | bytes 589824 | tf_op jit(solution)/shard_map/all_to_all | solution.py:124
  20.4 14.2 %all-to-all-done = bf16[16,8,1152]{2,1,0:T(8,128)(2,1)S(1)} async-done(((bf16[16,8,1152]{2,1,0:T(8,128)(2,1)}), bf16[16,8,1152]{2,1,0:T(8,128)(2,1)S(1)}, u32[]{:S(2)}, u32[]{:S(2)}) %all-to-all-start) | async-done | bytes 294944 | tf_op jit(solution)/shard_map/all_to_all | solution.py:124
  34.6 1.1 %obs.1 = (bf16[272,128]{1,0:T(8,128)(2,1)S(1)}, bf16[128,1024]{1,0:T(8,128)(2,1)S(1)}) custom-call(s32[1]{0:T(128)} %bitcast.2.which_ref, s32[16]{0:T(128)} %count_ref.1, bf16[128,1152]{1,0:T(8,128)(2,1)S(1)} %bitcast.10, f32[16,128]{1,0:T(8,128)} %bitcast.15, f32[16,128]{1,0:T(8,128)} %bitcast.16, s32[16,128]{1,0:T(8,128)} %bitcast.17), custom_call_target="tpu_custom_call" | custom-call | tf_op jit(solution)/shard_map/obs/pallas_call | solution.py:75
  35.7 7.8 %collective-permute-start = (bf16[272,128]{1,0:T(8,128)(2,1)S(1)}, bf16[272,128]{1,0:T(8,128)(2,1)S(1)}, u32[]{:S(2)}, u32[]{:S(2)}) collective-permute-start(bf16[272,128]{1,0:T(8,128)(2,1)S(1)} %get-tuple-element.8.sent_ref), channel_id=1, source_target_pairs={{0,1},{1,2},{2,3},{3,4},{4,5},{5,6},{6,7},{7,8},{8,9},{9,10},{10,1... | collective-permute-start | bytes 208904 | tf_op jit(solution)/shard_map/ppermute | solution.py:130
  43.5 6.2 %collective-permute-start.1 = (bf16[272,128]{1,0:T(8,128)(2,1)S(1)}, bf16[272,128]{1,0:T(8,128)(2,1)S(1)}, u32[]{:S(2)}, u32[]{:S(2)}) collective-permute-start(bf16[272,128]{1,0:T(8,128)(2,1)S(1)} %get-tuple-element.8.sent_ref), channel_id=1, source_target_pairs={{1,0},{2,1},{3,2},{4,3},{5,4},{6,5},{7,6},{8,7},{9,8},{10,9},{11,1... | collective-permute-start | bytes 208904 | tf_op jit(solution)/shard_map/ppermute | solution.py:131
  49.6 0.5 own.1.so_far_ref
  50.1 0.0 collective-permute-done.low_ref
  50.1 1.4 %collective-permute-done.1.high_ref = bf16[272,128]{1,0:T(8,128)(2,1)S(1)} collective-permute-done((bf16[272,128]{1,0:T(8,128)(2,1)S(1)}, bf16[272,128]{1,0:T(8,128)(2,1)S(1)}, u32[]{:S(2)}, u32[]{:S(2)}) %collective-permute-start.1) | collective-permute-done | bytes 69664 | tf_op jit(solution)/shard_map/ppermute | solution.py:131
  51.5 0.6 side.1
  52.1 26.1 %all_to_all.10 = bf16[16,8,1024]{2,1,0:T(8,128)(2,1)S(1)} all-to-all(bf16[16,8,1024]{2,1,0:T(8,128)(2,1)S(1)} %bitcast.12), channel_id=1, replica_groups=mesh['cell'=64,'mem'=16] {'mem'}, dimensions={0} | all-to-all | bytes 524288 | tf_op jit(solution)/shard_map/all_to_all | solution.py:139
  78.3 0.7 copy.9
Async XLA Ops:
  1.8 32.8 %all-to-all-start = ((bf16[16,8,1152]{2,1,0:T(8,128)(2,1)}), bf16[16,8,1152]{2,1,0:T(8,128)(2,1)S(1)}, u32[]{:S(2)}, u32[]{:S(2)}) async-start(bf16[16,8,1152]{2,1,0:T(8,128)(2,1)} %pack.1), calls=%async_computation | async-start | bytes 589824 | tf_op jit(solution)/shard_map/all_to_all | solution.py:124
  35.7 14.4 %collective-permute-start = (bf16[272,128]{1,0:T(8,128)(2,1)S(1)}, bf16[272,128]{1,0:T(8,128)(2,1)S(1)}, u32[]{:S(2)}, u32[]{:S(2)}) collective-permute-start(bf16[272,128]{1,0:T(8,128)(2,1)S(1)} %get-tuple-element.8.sent_ref), channel_id=1, source_target_pairs={{0,1},{1,2},{2,3},{3,4},{4,5},{5,6},{6,7},{7,8},{8,9},{9,10},{10,1... | collective-permute-start | bytes 208904 | tf_op jit(solution)/shard_map/ppermute | solution.py:130
  43.5 8.1 %collective-permute-start.1 = (bf16[272,128]{1,0:T(8,128)(2,1)S(1)}, bf16[272,128]{1,0:T(8,128)(2,1)S(1)}, u32[]{:S(2)}, u32[]{:S(2)}) collective-permute-start(bf16[272,128]{1,0:T(8,128)(2,1)S(1)} %get-tuple-element.8.sent_ref), channel_id=1, source_target_pairs={{1,0},{2,1},{3,2},{4,3},{5,4},{6,5},{7,6},{8,7},{9,8},{10,9},{11,1... | collective-permute-start | bytes 208904 | tf_op jit(solution)/shard_map/ppermute | solution.py:131

commit v3 on v1

v3 whole, which is shorter than its diff:
```python
import jax
import jax.numpy as jnp
from jax import lax
from jax.experimental import pallas as pl
from jax.experimental.pallas import tpu as pltpu
from jax.sharding import PartitionSpec as P

MEMBERS = 128
C_TILE = 1024
OBS_CAP = 128
NOISE = 512
LOCALIZE = 1024
LANES = 128
CHUNK = 256
POS_BASE = 32
SENT_ROWS = 2 * MEMBERS + 16
F32 = jnp.float32
BF16 = jnp.bfloat16
ANY = pl.BlockSpec(memory_space=pl.ANY)
SMEM = pl.BlockSpec(memory_space=pltpu.SMEM)
VMEM = pl.BlockSpec(memory_space=pltpu.VMEM)


def here(x):
    return pltpu.with_memory_space_constraint(x, pltpu.VMEM)


def pack_kernel(state_ref, noise_ref, pick_ref, out_ref, noise, pick, chosen, small, large, back):
    tiles, mem_dev, _ = out_ref.shape
    needed = [
        pltpu.make_async_copy(noise_ref, noise, small.at[0]),
        pltpu.make_async_copy(pick_ref, pick, small.at[1]),
    ]
    for copy in needed:
        copy.start()
    moved = [
        pltpu.make_async_copy(
            state_ref.at[:, t * C_TILE : (t + 1) * C_TILE],
            out_ref.at[t, :, 0:C_TILE],
            large.at[t],
        )
        for t in range(tiles)
    ]
    for copy in moved:
        copy.start()
    for copy in needed:
        copy.wait()
    table = [noise[:, k * LANES : (k + 1) * LANES] for k in range(NOISE // LANES)]
    for t in range(tiles):
        index = jnp.broadcast_to(pick[t : t + 1, :], (mem_dev, OBS_CAP))
        lane, block = index % LANES, index // LANES
        value = jnp.take_along_axis(table[0], lane, axis=1)
        for k in range(1, len(table)):
            value = jnp.where(block == k, jnp.take_along_axis(table[k], lane, axis=1), value)
        chosen[t] = value.astype(BF16)
    last = pltpu.make_async_copy(chosen, out_ref.at[:, :, C_TILE : C_TILE + OBS_CAP], back)
    last.start()
    for copy in moved:
        copy.wait()
    last.wait()


def pack(state, noise_table, picks):
    mem_dev = state.shape[0]
    tiles = picks.shape[0]
    return pl.pallas_call(
        pack_kernel,
        in_specs=[ANY, ANY, ANY],
        out_specs=ANY,
        out_shape=jax.ShapeDtypeStruct((tiles, mem_dev, C_TILE + OBS_CAP), BF16),
        scratch_shapes=[
            pltpu.VMEM((mem_dev, NOISE), F32),
            pltpu.VMEM((tiles, OBS_CAP), jnp.int32),
            pltpu.VMEM((tiles, mem_dev, OBS_CAP), BF16),
            pltpu.SemaphoreType.DMA((2,)),
            pltpu.SemaphoreType.DMA((tiles,)),
            pltpu.SemaphoreType.DMA,
        ],
        name="pack",
    )(state, noise_table, picks)


def ready_kernel(which_ref, count_ref, value_ref, error_ref, cell_ref, hot_ref, row_ref, pos_ref):
    me = which_ref[0]
    error = error_ref[pl.ds(me, 1), :]
    cell = cell_ref[pl.ds(me, 1), :]
    live = lax.broadcasted_iota(jnp.int32, (1, OBS_CAP), 1) < count_ref[me]
    row_ref[0:1, :] = value_ref[pl.ds(me, 1), :]
    row_ref[1:2, :] = error
    row_ref[2:3, :] = jnp.sqrt(error)
    row_ref[3:4, :] = live.astype(F32)
    row_ref[4:8, :] = jnp.zeros((4, OBS_CAP), F32)
    cells = lax.broadcasted_iota(jnp.int32, (C_TILE, OBS_CAP), 0)
    hot_ref[...] = (cells == cell).astype(F32).astype(BF16)
    row = lax.broadcasted_iota(jnp.int32, (16, OBS_CAP), 0)
    digits = jnp.where(row == 0, cell // POS_BASE, cell % POS_BASE)
    pos_ref[...] = jnp.where(row == 2, me % 2, digits).astype(F32).astype(BF16)


def obs_kernel(tile_ref, hot_ref, row_ref, pos_ref, send_ref):
    value, error, root, live = (row_ref[k : k + 1, :] for k in range(4))
    at_obs = jnp.dot(tile_ref[:, 0:C_TILE], hot_ref[...], preferred_element_type=F32)
    perturb = tile_ref[:, C_TILE : C_TILE + OBS_CAP].astype(F32)
    mean_at = jnp.sum(at_obs, axis=0, keepdims=True) / MEMBERS
    spread = (jnp.sum(at_obs * at_obs, axis=0, keepdims=True) - MEMBERS * mean_at * mean_at) / (
        MEMBERS - 1
    )
    weight = live / (spread + error)
    innovation = (value + root * perturb - at_obs) * weight
    send_ref[0:MEMBERS, :] = ((at_obs - mean_at) * live).astype(BF16)
    send_ref[MEMBERS : 2 * MEMBERS, :] = innovation.astype(BF16)
    send_ref[2 * MEMBERS : SENT_ROWS, :] = pos_ref[...]


def slots_of(sent_ref, side):
    digits = sent_ref[2 * MEMBERS : SENT_ROWS, :].astype(F32)
    shift = (2.0 * digits[2:3, :] - 1.0) * float(side * C_TILE)
    position = digits[0:1, :] * POS_BASE + digits[1:2, :] + shift
    position = jnp.transpose(jnp.broadcast_to(position, (OBS_CAP, OBS_CAP)))
    wide = jnp.concatenate([position] * (CHUNK // OBS_CAP), axis=1)
    return sent_ref[0:MEMBERS, :], sent_ref[MEMBERS : 2 * MEMBERS, :], wide


def increment_of(anom, slots, start):
    obs_anom, innovation, position = slots
    covariance = lax.dot_general(
        obs_anom, anom, (((0,), (0,)), ((), ())), preferred_element_type=F32
    )
    cells = lax.broadcasted_iota(jnp.int32, (OBS_CAP, CHUNK), 1).astype(F32) + float(start)
    away = cells - position
    inner = jnp.maximum(1.0 - (away * away) * (1.0 / (LOCALIZE * LOCALIZE)), 0.0)
    gain = (inner * inner * (covariance * (1.0 / (MEMBERS - 1)))).astype(BF16)
    return jnp.dot(innovation, gain, preferred_element_type=F32)


def own_kernel(tile_ref, sent_ref, anom_ref, out_ref):
    slots = slots_of(sent_ref, 0)
    for start in range(0, C_TILE, CHUNK):
        cut = slice(start, start + CHUNK)
        state = tile_ref[:, cut].astype(F32)
        anom = (state - jnp.sum(state, axis=0, keepdims=True) / MEMBERS).astype(BF16)
        anom_ref[:, cut] = anom
        out_ref[:, cut] = state + increment_of(anom, slots, start)


def side_kernel(so_far_ref, anom_ref, near_ref, far_ref, out_ref):
    near = slots_of(near_ref, 1)
    far = slots_of(far_ref, -1)
    for start in range(0, C_TILE, CHUNK):
        cut = slice(start, start + CHUNK)
        anom = anom_ref[:, cut]
        total = so_far_ref[:, cut]
        total = total + increment_of(anom, near, start) + increment_of(anom, far, start)
        out_ref[:, cut] = total.astype(BF16)


def swapped(x, first):
    axes = ("cell", "mem")
    count = lax.axis_size("cell") * lax.axis_size("mem")
    pairs = [(i, i + 1) for i in range(first, count - 1, 2)]
    return lax.ppermute(x, axes, pairs + [(j, i) for i, j in pairs])


def body(state, obs_value, obs_error, obs_cell, obs_count, obs_noise, noise_table):
    mem_dev, cell_count = state.shape
    tiles = cell_count // C_TILE
    rows = lambda a: a.reshape(tiles, OBS_CAP)
    which = lax.axis_index("mem").reshape(1)
    packed = pack(state, noise_table, rows(obs_noise))
    tile = lax.all_to_all(packed, "mem", split_axis=0, concat_axis=0, tiled=True)
    tile = tile.reshape(MEMBERS, C_TILE + OBS_CAP)
    hot, numbers, digits = pl.pallas_call(
        ready_kernel,
        in_specs=[SMEM, SMEM, VMEM, VMEM, VMEM],
        out_shape=(
            pltpu.VMEM((C_TILE, OBS_CAP), BF16),
            pltpu.VMEM((8, OBS_CAP), F32),
            pltpu.VMEM((16, OBS_CAP), BF16),
        ),
        name="ready",
    )(which, obs_count, rows(obs_value), rows(obs_error), rows(obs_cell))
    sent = pl.pallas_call(
        obs_kernel, out_shape=pltpu.VMEM((SENT_ROWS, OBS_CAP), BF16), name="obs"
    )(here(tile), here(hot), here(numbers), here(digits))
    near = swapped(sent, 0)
    far = swapped(sent, 1)
    anom, so_far = pl.pallas_call(
        own_kernel,
        out_shape=(pltpu.VMEM((MEMBERS, C_TILE), BF16), pltpu.VMEM((MEMBERS, C_TILE), F32)),
        name="own",
    )(here(tile), here(sent))
    analysis = pl.pallas_call(
        side_kernel, out_shape=pltpu.VMEM((MEMBERS, C_TILE), BF16), name="side"
    )(here(so_far), here(anom), here(near), here(far))
    returned = lax.all_to_all(
        analysis.reshape(tiles, mem_dev, C_TILE), "mem", split_axis=0, concat_axis=0, tiled=True
    )
    return jnp.transpose(returned, (1, 0, 2)).reshape(mem_dev, cell_count)


def solution(mesh):
    placed = (
        P("mem", "cell"),
        P("cell"),
        P("cell"),
        P("cell"),
        P("cell"),
        P("cell"),
        P("mem", None),
    )
    return jax.shard_map(
        body, mesh=mesh, in_specs=placed, out_specs=P("mem", "cell"), check_vma=False
    )
```

time: 83.8 us -> 83.7 us (level)
  the two profiles are of different devices: /device:TPU:31 before, /device:TPU:30 now
where the time goes in v3:
time: 83.7 us; the launch traced here: 83.2 us
  waiting for transfers between devices  24.3 us (29%)
  starting transfers between devices  24 us (29%)
  blocking collectives  22.7 us (27%)
  Pallas kernels  11.4 us (14%)
    all_to_all x1, blocking collectives, body(): lax.all_to_all(analysis.reshape(tiles, mem_dev, C_TILE), 'mem', split_axi...  22.7 us
    all_to_all x1, starting transfers between devices, body(): lax.all_to_all(packed, 'mem', split_axis=0, concat_axis=0, tiled=True)  18.9 us
    all_to_all x1, waiting for transfers between devices, body(): lax.all_to_all(packed, 'mem', split_axis=0, concat_axis=0, tiled=True)  18.5 us
    pallas_call x1, Pallas kernels, pack(): pl.pallas_call(pack_kernel, in_specs=[ANY, ANY, ANY], out_specs=ANY, out_...  9.21 us
    ppermute x2, waiting for transfers between devices, swapped(): return lax.ppermute(x, axes, pairs + [(j, i) for i, j in pairs])  5.8 us
    ppermute x2, starting transfers between devices, swapped(): return lax.ppermute(x, axes, pairs + [(j, i) for i, j in pairs])  5.17 us
  transfers between devices with their start and end apart: 3, of which 3 were waited for; matrix products, arithmetic and copies ran while one was open for 0% of the time, Pallas kernels for 2%

profile of v3, /device:TPU:30, one launch (start us, length us, event | category | flops | bytes accessed | tf_op | source)
XLA Modules:
  0.0 83.2 jit_solution(14158177890595501690)
XLA Ops:
  0.0 9.2 %pack.1 = bf16[16,8,1152]{2,1,0:T(8,128)(2,1)} custom-call(bf16[8,16384]{1,0:T(8,128)(2,1)} %state_ref.1, f32[8,512]{1,0:T(8,128)} %noise_ref.1, s32[16,128]{1,0:T(8,128)} %bitcast.14), custom_call_target="tpu_custom_call" | custom-call | tf_op jit(solution)/shard_map/pack/pallas_call | solution.py:66
  9.2 18.9 %all-to-all-start = ((bf16[16,8,1152]{2,1,0:T(8,128)(2,1)}), bf16[16,8,1152]{2,1,0:T(8,128)(2,1)S(1)}, u32[]{:S(2)}, u32[]{:S(2)}) async-start(bf16[16,8,1152]{2,1,0:T(8,128)(2,1)} %pack.1), calls=%async_computation | async-start | bytes 589824 | tf_op jit(solution)/shard_map/all_to_all | solution.py:170
  28.1 0.9 %ready.1 = (bf16[1024,128]{1,0:T(8,128)(2,1)S(1)}, f32[8,128]{1,0:T(8,128)S(1)}, bf16[16,128]{1,0:T(8,128)(2,1)S(1)}) custom-call(s32[1]{0:T(128)} %bitcast.2.which_ref, s32[16]{0:T(128)} %count_ref.1, f32[16,128]{1,0:T(8,128)} %bitcast.15, f32[16,128]{1,0:T(8,128)} %bitcast.16, s32[16,128]{1,0:T(8,128)} %bitcast.17), custom_call_target="tpu_custom_call" | custom-call | tf_op jit(solution)/shard_map/ready/pallas_call | solution.py:172
  29.0 18.5 %all-to-all-done = bf16[16,8,1152]{2,1,0:T(8,128)(2,1)S(1)} async-done(((bf16[16,8,1152]{2,1,0:T(8,128)(2,1)}), bf16[16,8,1152]{2,1,0:T(8,128)(2,1)S(1)}, u32[]{:S(2)}, u32[]{:S(2)}) %all-to-all-start) | async-done | bytes 294944 | tf_op jit(solution)/shard_map/all_to_all | solution.py:170
  47.5 0.2 obs.1.sent_ref
  47.7 3.2 %collective-permute-start = (bf16[272,128]{1,0:T(8,128)(2,1)S(1)}, bf16[272,128]{1,0:T(8,128)(2,1)S(1)}, u32[]{:S(2)}, u32[]{:S(2)}) collective-permute-start(bf16[272,128]{1,0:T(8,128)(2,1)S(1)} %obs.1.sent_ref), channel_id=1, source_target_pairs={{0,1},{2,3},{4,5},{6,7},{8,9},{10,11},{12,13},{14,15},{16,17},{18,... | collective-permute-start | bytes 208904 | tf_op jit(solution)/shard_map/ppermute | solution.py:161
  51.0 1.9 %collective-permute-start.1 = (bf16[272,128]{1,0:T(8,128)(2,1)S(1)}, bf16[272,128]{1,0:T(8,128)(2,1)S(1)}, u32[]{:S(2)}, u32[]{:S(2)}) collective-permute-start(bf16[272,128]{1,0:T(8,128)(2,1)S(1)} %obs.1.sent_ref), channel_id=1, source_target_pairs={{1,2},{3,4},{5,6},{7,8},{9,10},{11,12},{13,14},{15,16},{17,18},{19... | collective-permute-start | bytes 208904 | tf_op jit(solution)/shard_map/ppermute | solution.py:161
  52.9 0.5 own.1
  53.4 0.5 collective-permute-done.near_ref
  53.9 5.3 %collective-permute-done.1.far_ref = bf16[272,128]{1,0:T(8,128)(2,1)S(1)} collective-permute-done((bf16[272,128]{1,0:T(8,128)(2,1)S(1)}, bf16[272,128]{1,0:T(8,128)(2,1)S(1)}, u32[]{:S(2)}, u32[]{:S(2)}) %collective-permute-start.1) | collective-permute-done | bytes 69664 | tf_op jit(solution)/shard_map/ppermute | solution.py:161
  59.2 0.6 side.1
  59.8 22.7 %all_to_all.10 = bf16[16,8,1024]{2,1,0:T(8,128)(2,1)S(1)} all-to-all(bf16[16,8,1024]{2,1,0:T(8,128)(2,1)S(1)} %bitcast.12), channel_id=1, replica_groups=mesh['cell'=64,'mem'=16] {'mem'}, dimensions={0} | all-to-all | bytes 524288 | tf_op jit(solution)/shard_map/all_to_all | solution.py:195
  82.5 0.7 copy.9
Async XLA Ops:
  9.2 38.3 %all-to-all-start = ((bf16[16,8,1152]{2,1,0:T(8,128)(2,1)}), bf16[16,8,1152]{2,1,0:T(8,128)(2,1)S(1)}, u32[]{:S(2)}, u32[]{:S(2)}) async-start(bf16[16,8,1152]{2,1,0:T(8,128)(2,1)} %pack.1), calls=%async_computation | async-start | bytes 589824 | tf_op jit(solution)/shard_map/all_to_all | solution.py:170
  47.7 6.2 %collective-permute-start = (bf16[272,128]{1,0:T(8,128)(2,1)S(1)}, bf16[272,128]{1,0:T(8,128)(2,1)S(1)}, u32[]{:S(2)}, u32[]{:S(2)}) collective-permute-start(bf16[272,128]{1,0:T(8,128)(2,1)S(1)} %obs.1.sent_ref), channel_id=1, source_target_pairs={{0,1},{2,3},{4,5},{6,7},{8,9},{10,11},{12,13},{14,15},{16,17},{18,... | collective-permute-start | bytes 208904 | tf_op jit(solution)/shard_map/ppermute | solution.py:161
  51.0 8.2 %collective-permute-start.1 = (bf16[272,128]{1,0:T(8,128)(2,1)S(1)}, bf16[272,128]{1,0:T(8,128)(2,1)S(1)}, u32[]{:S(2)}, u32[]{:S(2)}) collective-permute-start(bf16[272,128]{1,0:T(8,128)(2,1)S(1)} %obs.1.sent_ref), channel_id=1, source_target_pairs={{1,2},{3,4},{5,6},{7,8},{9,10},{11,12},{13,14},{15,16},{17,18},{19... | collective-permute-start | bytes 208904 | tf_op jit(solution)/shard_map/ppermute | solution.py:161

commit v4 on v3

--- a/solution.py
+++ b/solution.py
@@ -25,63 +25,40 @@
     return pltpu.with_memory_space_constraint(x, pltpu.VMEM)
 
 
-def pack_kernel(state_ref, noise_ref, pick_ref, out_ref, noise, pick, chosen, small, large, back):
+def place_of(tile, flipped, tiles):
+    return tile + flipped * (tiles - 1 - 2 * tile)
+
+
+def spot_of(device, tiles):
+    flipped = lax.rem(lax.div(device, tiles), 2)
+    return place_of(lax.rem(device, tiles), flipped, tiles), flipped
+
+
+def prepare_kernel(
+    where_ref, count_ref, state_ref, noise_ref, pick_ref, value_ref, error_ref, cell_ref,
+    out_ref, hot_ref, row_ref, pos_ref, sem,
+):
     tiles, mem_dev, _ = out_ref.shape
-    needed = [
-        pltpu.make_async_copy(noise_ref, noise, small.at[0]),
-        pltpu.make_async_copy(pick_ref, pick, small.at[1]),
-    ]
-    for copy in needed:
-        copy.start()
+    me, flipped = spot_of(where_ref[0], tiles)
+    places = [place_of(t, flipped, tiles) for t in range(tiles)]
     moved = [
         pltpu.make_async_copy(
             state_ref.at[:, t * C_TILE : (t + 1) * C_TILE],
-            out_ref.at[t, :, 0:C_TILE],
-            large.at[t],
+            out_ref.at[places[t], :, 0:C_TILE],
+            sem.at[t],
         )
         for t in range(tiles)
     ]
     for copy in moved:
         copy.start()
-    for copy in needed:
-        copy.wait()
-    table = [noise[:, k * LANES : (k + 1) * LANES] for k in range(NOISE // LANES)]
+    table = [noise_ref[:, k * LANES : (k + 1) * LANES] for k in range(NOISE // LANES)]
     for t in range(tiles):
-        index = jnp.broadcast_to(pick[t : t + 1, :], (mem_dev, OBS_CAP))
+        index = jnp.broadcast_to(pick_ref[t : t + 1, :], (mem_dev, OBS_CAP))
         lane, block = index % LANES, index // LANES
         value = jnp.take_along_axis(table[0], lane, axis=1)
         for k in range(1, len(table)):
             value = jnp.where(block == k, jnp.take_along_axis(table[k], lane, axis=1), value)
-        chosen[t] = value.astype(BF16)
-    last = pltpu.make_async_copy(chosen, out_ref.at[:, :, C_TILE : C_TILE + OBS_CAP], back)
-    last.start()
-    for copy in moved:
-        copy.wait()
-    last.wait()
-
-
-def pack(state, noise_table, picks):
-    mem_dev = state.shape[0]
-    tiles = picks.shape[0]
-    return pl.pallas_call(
-        pack_kernel,
-        in_specs=[ANY, ANY, ANY],
-        out_specs=ANY,
-        out_shape=jax.ShapeDtypeStruct((tiles, mem_dev, C_TILE + OBS_CAP), BF16),
-        scratch_shapes=[
-            pltpu.VMEM((mem_dev, NOISE), F32),
-            pltpu.VMEM((tiles, OBS_CAP), jnp.int32),
-            pltpu.VMEM((tiles, mem_dev, OBS_CAP), BF16),
-            pltpu.SemaphoreType.DMA((2,)),
-            pltpu.SemaphoreType.DMA((tiles,)),
-            pltpu.SemaphoreType.DMA,
-        ],
-        name="pack",
-    )(state, noise_table, picks)
-
-
-def ready_kernel(which_ref, count_ref, value_ref, error_ref, cell_ref, hot_ref, row_ref, pos_ref):
-    me = which_ref[0]
+        out_ref[places[t], :, C_TILE : C_TILE + OBS_CAP] = value.astype(BF16)
     error = error_ref[pl.ds(me, 1), :]
     cell = cell_ref[pl.ds(me, 1), :]
     live = lax.broadcasted_iota(jnp.int32, (1, OBS_CAP), 1) < count_ref[me]
@@ -94,7 +71,26 @@
     hot_ref[...] = (cells == cell).astype(F32).astype(BF16)
     row = lax.broadcasted_iota(jnp.int32, (16, OBS_CAP), 0)
     digits = jnp.where(row == 0, cell // POS_BASE, cell % POS_BASE)
-    pos_ref[...] = jnp.where(row == 2, me % 2, digits).astype(F32).astype(BF16)
+    pos_ref[...] = jnp.where(row == 2, lax.rem(me, 2), digits).astype(F32).astype(BF16)
+    for copy in moved:
+        copy.wait()
+
+
+def restore_kernel(where_ref, back_ref, out_ref, sem):
+    tiles = back_ref.shape[0]
+    _, flipped = spot_of(where_ref[0], tiles)
+    moved = [
+        pltpu.make_async_copy(
+            back_ref.at[place_of(t, flipped, tiles)],
+            out_ref.at[:, t * C_TILE : (t + 1) * C_TILE],
+            sem.at[t],
+        )
+        for t in range(tiles)
+    ]
+    for copy in moved:
+        copy.start()
+    for copy in moved:
+        copy.wait()
 
 
 def obs_kernel(tile_ref, hot_ref, row_ref, pos_ref, send_ref):
@@ -155,30 +151,38 @@
 
 
 def swapped(x, first):
-    axes = ("cell", "mem")
-    count = lax.axis_size("cell") * lax.axis_size("mem")
-    pairs = [(i, i + 1) for i in range(first, count - 1, 2)]
-    return lax.ppermute(x, axes, pairs + [(j, i) for i, j in pairs])
+    shards, tiles = lax.axis_size("cell"), lax.axis_size("mem")
+    line = [
+        shard * tiles + place_of(tile, shard % 2, tiles)
+        for shard in range(shards)
+        for tile in range(tiles)
+    ]
+    pairs = [(line[i], line[i + 1]) for i in range(first, len(line) - 1, 2)]
+    return lax.ppermute(x, ("cell", "mem"), pairs + [(j, i) for i, j in pairs])
 
 
 def body(state, obs_value, obs_error, obs_cell, obs_count, obs_noise, noise_table):
     mem_dev, cell_count = state.shape
     tiles = cell_count // C_TILE
     rows = lambda a: a.reshape(tiles, OBS_CAP)
-    which = lax.axis_index("mem").reshape(1)
-    packed = pack(state, noise_table, rows(obs_noise))
-    tile = lax.all_to_all(packed, "mem", split_axis=0, concat_axis=0, tiled=True)
-    tile = tile.reshape(MEMBERS, C_TILE + OBS_CAP)
-    hot, numbers, digits = pl.pallas_call(
-        ready_kernel,
-        in_specs=[SMEM, SMEM, VMEM, VMEM, VMEM],
+    where = lax.axis_index(("cell", "mem")).reshape(1)
+    packed, hot, numbers, digits = pl.pallas_call(
+        prepare_kernel,
+        in_specs=[SMEM, SMEM, ANY, VMEM, VMEM, VMEM, VMEM, VMEM],
         out_shape=(
+            pltpu.VMEM((tiles, mem_dev, C_TILE + OBS_CAP), BF16),
             pltpu.VMEM((C_TILE, OBS_CAP), BF16),
             pltpu.VMEM((8, OBS_CAP), F32),
             pltpu.VMEM((16, OBS_CAP), BF16),
         ),
-        name="ready",
-    )(which, obs_count, rows(obs_value), rows(obs_error), rows(obs_cell))
+        scratch_shapes=[pltpu.SemaphoreType.DMA((tiles,))],
+        name="prepare",
+    )(
+        where, obs_count, state, noise_table,
+        rows(obs_noise), rows(obs_value), rows(obs_error), rows(obs_cell),
+    )
+    tile = lax.all_to_all(packed, "mem", split_axis=0, concat_axis=0, tiled=True)
+    tile = tile.reshape(MEMBERS, C_TILE + OBS_CAP)
     sent = pl.pallas_call(
         obs_kernel, out_shape=pltpu.VMEM((SENT_ROWS, OBS_CAP), BF16), name="obs"
     )(here(tile), here(hot), here(numbers), here(digits))
@@ -195,7 +199,14 @@
     returned = lax.all_to_all(
         analysis.reshape(tiles, mem_dev, C_TILE), "mem", split_axis=0, concat_axis=0, tiled=True
     )
-    return jnp.transpose(returned, (1, 0, 2)).reshape(mem_dev, cell_count)
+    return pl.pallas_call(
+        restore_kernel,
+        in_specs=[SMEM, VMEM],
+        out_specs=ANY,
+        out_shape=jax.ShapeDtypeStruct((mem_dev, cell_count), BF16),
+        scratch_shapes=[pltpu.SemaphoreType.DMA((tiles,))],
+        name="restore",
+    )(where, here(returned))
 
 
 def solution(mesh):

time: 83.7 us -> 75.5 us (0.902)
  the two profiles are of different devices: /device:TPU:30 before, /device:TPU:62 now
where the time goes in v4:
time: 75.5 us; the launch traced here: 75 us
  blocking collectives  62.5 us (83%)
  starting transfers between devices  5.17 us (7%)
  Pallas kernels  4.02 us (5%)
  waiting for transfers between devices  3.23 us (4%)
    all_to_all x1, blocking collectives, body(): lax.all_to_all(packed, 'mem', split_axis=0, concat_axis=0, tiled=True)  38.1 us
    all_to_all x1, blocking collectives, body(): lax.all_to_all(analysis.reshape(tiles, mem_dev, C_TILE), 'mem', split_axi...  24.5 us
    ppermute x2, starting transfers between devices, swapped(): return lax.ppermute(x, ('cell', 'mem'), pairs + [(j, i) for i, j in pairs])  5.17 us
    ppermute x2, waiting for transfers between devices, swapped(): return lax.ppermute(x, ('cell', 'mem'), pairs + [(j, i) for i, j in pairs])  3.23 us
    pallas_call x1, Pallas kernels, body(): pl.pallas_call(prepare_kernel, in_specs=[SMEM, SMEM, ANY, VMEM, VMEM, VME...  1.87 us
  transfers between devices with their start and end apart: 2, of which 2 were waited for; matrix products, arithmetic and copies ran while one was open for 0% of the time, Pallas kernels for 1%

profile of v4, /device:TPU:62, one launch (start us, length us, event | category | flops | bytes accessed | tf_op | source)
XLA Modules:
  0.0 75.0 jit_solution(8684321962541678519)
XLA Ops:
  0.0 1.9 %prepare.1 = (bf16[16,8,1152]{2,1,0:T(8,128)(2,1)S(1)}, bf16[1024,128]{1,0:T(8,128)(2,1)S(1)}, f32[8,128]{1,0:T(8,128)S(1)}, bf16[16,128]{1,0:T(8,128)(2,1)S(1)}) custom-call(s32[1]{0:T(128)} %bitcast.where_ref, s32[16]{0:T(128)} %count_ref.1, bf16[8,16384]{1,0:T(8,128)(2,1)} %state_ref.1, f32[8,512]{1,0:T(8,128)} %noise_ref.1, s32[16,128]{1,0:T(8,128)} %bitcast.10, ...), custom_call_target="tpu_custom_call" | custom-call | tf_op jit(solution)/shard_map/prepare/pallas_call | solution.py:169
  1.9 38.1 %all_to_all.10 = bf16[16,8,1152]{2,1,0:T(8,128)(2,1)S(1)} all-to-all(bf16[16,8,1152]{2,1,0:T(8,128)(2,1)S(1)} %get-tuple-element.11), channel_id=1, replica_groups=mesh['cell'=64,'mem'=16] {'mem'}, dimensions={0} | all-to-all | bytes 589824 | tf_op jit(solution)/shard_map/all_to_all | solution.py:184
  39.9 0.2 obs.1.sent_ref
  40.2 3.2 %collective-permute-start = (bf16[272,128]{1,0:T(8,128)(2,1)S(1)}, bf16[272,128]{1,0:T(8,128)(2,1)S(1)}, u32[]{:S(2)}, u32[]{:S(2)}) collective-permute-start(bf16[272,128]{1,0:T(8,128)(2,1)S(1)} %obs.1.sent_ref), channel_id=1, source_target_pairs={{0,1},{2,3},{4,5},{6,7},{8,9},{10,11},{12,13},{14,15},{31,30},{29,... | collective-permute-start | bytes 208904 | tf_op jit(solution)/shard_map/ppermute | solution.py:161
  43.4 1.9 %collective-permute-start.1 = (bf16[272,128]{1,0:T(8,128)(2,1)S(1)}, bf16[272,128]{1,0:T(8,128)(2,1)S(1)}, u32[]{:S(2)}, u32[]{:S(2)}) collective-permute-start(bf16[272,128]{1,0:T(8,128)(2,1)S(1)} %obs.1.sent_ref), channel_id=1, source_target_pairs={{1,2},{3,4},{5,6},{7,8},{9,10},{11,12},{13,14},{15,31},{30,29},{28... | collective-permute-start | bytes 208904 | tf_op jit(solution)/shard_map/ppermute | solution.py:161
  45.4 0.5 own.1
  45.8 0.5 collective-permute-done.near_ref
  46.4 2.7 %collective-permute-done.1.far_ref = bf16[272,128]{1,0:T(8,128)(2,1)S(1)} collective-permute-done((bf16[272,128]{1,0:T(8,128)(2,1)S(1)}, bf16[272,128]{1,0:T(8,128)(2,1)S(1)}, u32[]{:S(2)}, u32[]{:S(2)}) %collective-permute-start.1) | collective-permute-done | bytes 69664 | tf_op jit(solution)/shard_map/ppermute | solution.py:161
  49.1 0.6 side.1
  49.7 24.5 %all_to_all.11.back_ref = bf16[16,8,1024]{2,1,0:T(8,128)(2,1)S(1)} all-to-all(bf16[16,8,1024]{2,1,0:T(8,128)(2,1)S(1)} %bitcast.9), channel_id=1, replica_groups=mesh['cell'=64,'mem'=16] {'mem'}, dimensions={0} | all-to-all | bytes 524288 | tf_op jit(solution)/shard_map/all_to_all | solution.py:199
  74.2 0.8 %restore.1 = bf16[8,16384]{1,0:T(8,128)(2,1)} custom-call(s32[1]{0:T(128)} %bitcast.where_ref, bf16[16,8,1024]{2,1,0:T(8,128)(2,1)S(1)} %all_to_all.11.back_ref), custom_call_target="tpu_custom_call" | custom-call | tf_op jit(solution)/shard_map/restore/pallas_call | solution.py:202
Async XLA Ops:
  40.2 6.2 %collective-permute-start = (bf16[272,128]{1,0:T(8,128)(2,1)S(1)}, bf16[272,128]{1,0:T(8,128)(2,1)S(1)}, u32[]{:S(2)}, u32[]{:S(2)}) collective-permute-start(bf16[272,128]{1,0:T(8,128)(2,1)S(1)} %obs.1.sent_ref), channel_id=1, source_target_pairs={{0,1},{2,3},{4,5},{6,7},{8,9},{10,11},{12,13},{14,15},{31,30},{29,... | collective-permute-start | bytes 208904 | tf_op jit(solution)/shard_map/ppermute | solution.py:161
  43.4 5.6 %collective-permute-start.1 = (bf16[272,128]{1,0:T(8,128)(2,1)S(1)}, bf16[272,128]{1,0:T(8,128)(2,1)S(1)}, u32[]{:S(2)}, u32[]{:S(2)}) collective-permute-start(bf16[272,128]{1,0:T(8,128)(2,1)S(1)} %obs.1.sent_ref), channel_id=1, source_target_pairs={{1,2},{3,4},{5,6},{7,8},{9,10},{11,12},{13,14},{15,31},{30,29},{28... | collective-permute-start | bytes 208904 | tf_op jit(solution)/shard_map/ppermute | solution.py:161

commit v5 on v4

--- a/solution.py
+++ b/solution.py
@@ -4,6 +4,7 @@
 from jax.experimental import pallas as pl
 from jax.experimental.pallas import tpu as pltpu
 from jax.sharding import PartitionSpec as P
+
 
 MEMBERS = 128
 C_TILE = 1024
@@ -17,8 +18,6 @@
 F32 = jnp.float32
 BF16 = jnp.bfloat16
 ANY = pl.BlockSpec(memory_space=pl.ANY)
-SMEM = pl.BlockSpec(memory_space=pltpu.SMEM)
-VMEM = pl.BlockSpec(memory_space=pltpu.VMEM)
 
 
 def here(x):
@@ -35,15 +34,27 @@
 
 
 def prepare_kernel(
-    where_ref, count_ref, state_ref, noise_ref, pick_ref, value_ref, error_ref, cell_ref,
-    out_ref, hot_ref, row_ref, pos_ref, sem,
+    count_hbm, state_hbm, noise_hbm, pick_hbm, value_hbm, error_hbm, cell_hbm,
+    out_ref, hot_ref, row_ref, pos_ref,
+    count_ref, noise_ref, pick_ref, value_ref, error_ref, cell_ref, sem, small,
 ):
     tiles, mem_dev, _ = out_ref.shape
-    me, flipped = spot_of(where_ref[0], tiles)
+    me, flipped = spot_of(lax.axis_index(("cell", "mem")), tiles)
     places = [place_of(t, flipped, tiles) for t in range(tiles)]
+    inputs = (
+        (noise_hbm, noise_ref),
+        (pick_hbm, pick_ref),
+        (cell_hbm, cell_ref),
+        (value_hbm, value_ref),
+        (error_hbm, error_ref),
+        (count_hbm, count_ref),
+    )
+    read = [pltpu.make_async_copy(a, b, small.at[k]) for k, (a, b) in enumerate(inputs)]
+    for copy in read:
+        copy.start()
     moved = [
         pltpu.make_async_copy(
-            state_ref.at[:, t * C_TILE : (t + 1) * C_TILE],
+            state_hbm.at[:, t * C_TILE : (t + 1) * C_TILE],
             out_ref.at[places[t], :, 0:C_TILE],
             sem.at[t],
         )
@@ -51,6 +62,8 @@
     ]
     for copy in moved:
         copy.start()
+    for copy in read[:2]:
+        copy.wait()
     table = [noise_ref[:, k * LANES : (k + 1) * LANES] for k in range(NOISE // LANES)]
     for t in range(tiles):
         index = jnp.broadcast_to(pick_ref[t : t + 1, :], (mem_dev, OBS_CAP))
@@ -59,6 +72,8 @@
         for k in range(1, len(table)):
             value = jnp.where(block == k, jnp.take_along_axis(table[k], lane, axis=1), value)
         out_ref[places[t], :, C_TILE : C_TILE + OBS_CAP] = value.astype(BF16)
+    for copy in read[2:]:
+        copy.wait()
     error = error_ref[pl.ds(me, 1), :]
     cell = cell_ref[pl.ds(me, 1), :]
     live = lax.broadcasted_iota(jnp.int32, (1, OBS_CAP), 1) < count_ref[me]
@@ -76,9 +91,9 @@
         copy.wait()
 
 
-def restore_kernel(where_ref, back_ref, out_ref, sem):
+def restore_kernel(back_ref, out_ref, sem):
     tiles = back_ref.shape[0]
-    _, flipped = spot_of(where_ref[0], tiles)
+    _, flipped = spot_of(lax.axis_index(("cell", "mem")), tiles)
     moved = [
         pltpu.make_async_copy(
             back_ref.at[place_of(t, flipped, tiles)],
@@ -165,20 +180,28 @@
     mem_dev, cell_count = state.shape
     tiles = cell_count // C_TILE
     rows = lambda a: a.reshape(tiles, OBS_CAP)
-    where = lax.axis_index(("cell", "mem")).reshape(1)
     packed, hot, numbers, digits = pl.pallas_call(
         prepare_kernel,
-        in_specs=[SMEM, SMEM, ANY, VMEM, VMEM, VMEM, VMEM, VMEM],
+        in_specs=[ANY] * 7,
         out_shape=(
             pltpu.VMEM((tiles, mem_dev, C_TILE + OBS_CAP), BF16),
             pltpu.VMEM((C_TILE, OBS_CAP), BF16),
             pltpu.VMEM((8, OBS_CAP), F32),
             pltpu.VMEM((16, OBS_CAP), BF16),
         ),
-        scratch_shapes=[pltpu.SemaphoreType.DMA((tiles,))],
+        scratch_shapes=[
+            pltpu.SMEM((tiles,), jnp.int32),
+            pltpu.VMEM((mem_dev, NOISE), F32),
+            pltpu.VMEM((tiles, OBS_CAP), jnp.int32),
+            pltpu.VMEM((tiles, OBS_CAP), F32),
+            pltpu.VMEM((tiles, OBS_CAP), F32),
+            pltpu.VMEM((tiles, OBS_CAP), jnp.int32),
+            pltpu.SemaphoreType.DMA((tiles,)),
+            pltpu.SemaphoreType.DMA((6,)),
+        ],
         name="prepare",
     )(
-        where, obs_count, state, noise_table,
+        obs_count, state, noise_table,
         rows(obs_noise), rows(obs_value), rows(obs_error), rows(obs_cell),
     )
     tile = lax.all_to_all(packed, "mem", split_axis=0, concat_axis=0, tiled=True)
@@ -186,8 +209,8 @@
     sent = pl.pallas_call(
         obs_kernel, out_shape=pltpu.VMEM((SENT_ROWS, OBS_CAP), BF16), name="obs"
     )(here(tile), here(hot), here(numbers), here(digits))
+    far = swapped(sent, 1)
     near = swapped(sent, 0)
-    far = swapped(sent, 1)
     anom, so_far = pl.pallas_call(
         own_kernel,
         out_shape=(pltpu.VMEM((MEMBERS, C_TILE), BF16), pltpu.VMEM((MEMBERS, C_TILE), F32)),
@@ -201,12 +224,11 @@
     )
     return pl.pallas_call(
         restore_kernel,
-        in_specs=[SMEM, VMEM],
         out_specs=ANY,
         out_shape=jax.ShapeDtypeStruct((mem_dev, cell_count), BF16),
         scratch_shapes=[pltpu.SemaphoreType.DMA((tiles,))],
         name="restore",
-    )(where, here(returned))
+    )(here(returned))
 
 
 def solution(mesh):

time: 75.5 us -> 74.7 us (0.989)
  the two profiles are of different devices: /device:TPU:62 before, /device:TPU:20 now
where the time goes in v5:
time: 74.7 us; the launch traced here: 74.3 us
  blocking collectives  62.5 us (84%)
  starting transfers between devices  5.17 us (7%)
  Pallas kernels  3.34 us (4%)
  waiting for transfers between devices  3.23 us (4%)
    all_to_all x1, blocking collectives, body(): lax.all_to_all(packed, 'mem', split_axis=0, concat_axis=0, tiled=True)  38.1 us
    all_to_all x1, blocking collectives, body(): lax.all_to_all(analysis.reshape(tiles, mem_dev, C_TILE), 'mem', split_axi...  24.5 us
    ppermute x2, starting transfers between devices, swapped(): return lax.ppermute(x, ('cell', 'mem'), pairs + [(j, i) for i, j in pairs])  5.17 us
    ppermute x2, waiting for transfers between devices, swapped(): return lax.ppermute(x, ('cell', 'mem'), pairs + [(j, i) for i, j in pairs])  3.23 us
  transfers between devices with their start and end apart: 2, of which 2 were waited for; matrix products, arithmetic and copies ran while one was open for 0% of the time, Pallas kernels for 1%

profile of v5, /device:TPU:20, one launch (start us, length us, event | category | flops | bytes accessed | tf_op | source)
XLA Modules:
  0.0 74.3 jit_solution(4737235209626444843)
XLA Ops:
  0.0 1.2 %prepare.1 = (bf16[16,8,1152]{2,1,0:T(8,128)(2,1)S(1)}, bf16[1024,128]{1,0:T(8,128)(2,1)S(1)}, f32[8,128]{1,0:T(8,128)S(1)}, bf16[16,128]{1,0:T(8,128)(2,1)S(1)}) custom-call(s32[16]{0:T(128)} %count_hbm.1, bf16[8,16384]{1,0:T(8,128)(2,1)} %state_hbm.1, f32[8,512]{1,0:T(8,128)} %noise_hbm.1, s32[16,128]{1,0:T(8,128)} %bitcast.9, f32[16,128]{1,0:T(8,128)} %bitcast.10, ...), custom_call_target="tpu_custom_call" | custom-call | tf_op jit(solution)/shard_map/prepare/pallas_call | solution.py:183
  1.2 38.1 %all_to_all.10 = bf16[16,8,1152]{2,1,0:T(8,128)(2,1)S(1)} all-to-all(bf16[16,8,1152]{2,1,0:T(8,128)(2,1)S(1)} %get-tuple-element.11), channel_id=1, replica_groups=mesh['cell'=64,'mem'=16] {'mem'}, dimensions={0} | all-to-all | bytes 589824 | tf_op jit(solution)/shard_map/all_to_all | solution.py:207
  39.2 0.3 obs.1.sent_ref
  39.5 3.2 %collective-permute-start = (bf16[272,128]{1,0:T(8,128)(2,1)S(1)}, bf16[272,128]{1,0:T(8,128)(2,1)S(1)}, u32[]{:S(2)}, u32[]{:S(2)}) collective-permute-start(bf16[272,128]{1,0:T(8,128)(2,1)S(1)} %obs.1.sent_ref), channel_id=1, source_target_pairs={{0,1},{2,3},{4,5},{6,7},{8,9},{10,11},{12,13},{14,15},{31,30},{29,... | collective-permute-start | bytes 208904 | tf_op jit(solution)/shard_map/ppermute | solution.py:176
  42.8 1.9 %collective-permute-start.1 = (bf16[272,128]{1,0:T(8,128)(2,1)S(1)}, bf16[272,128]{1,0:T(8,128)(2,1)S(1)}, u32[]{:S(2)}, u32[]{:S(2)}) collective-permute-start(bf16[272,128]{1,0:T(8,128)(2,1)S(1)} %obs.1.sent_ref), channel_id=1, source_target_pairs={{1,2},{3,4},{5,6},{7,8},{9,10},{11,12},{13,14},{15,31},{30,29},{28... | collective-permute-start | bytes 208904 | tf_op jit(solution)/shard_map/ppermute | solution.py:176
  44.7 0.5 own.1
  45.2 0.5 collective-permute-done.near_ref
  45.7 2.7 %collective-permute-done.1.far_ref = bf16[272,128]{1,0:T(8,128)(2,1)S(1)} collective-permute-done((bf16[272,128]{1,0:T(8,128)(2,1)S(1)}, bf16[272,128]{1,0:T(8,128)(2,1)S(1)}, u32[]{:S(2)}, u32[]{:S(2)}) %collective-permute-start.1) | collective-permute-done | bytes 69664 | tf_op jit(solution)/shard_map/ppermute | solution.py:176
  48.4 0.6 side.1
  49.0 24.5 %all_to_all.11.back_ref = bf16[16,8,1024]{2,1,0:T(8,128)(2,1)S(1)} all-to-all(bf16[16,8,1024]{2,1,0:T(8,128)(2,1)S(1)} %bitcast.8), channel_id=1, replica_groups=mesh['cell'=64,'mem'=16] {'mem'}, dimensions={0} | all-to-all | bytes 524288 | tf_op jit(solution)/shard_map/all_to_all | solution.py:222
  73.5 0.8 %restore.1 = bf16[8,16384]{1,0:T(8,128)(2,1)} custom-call(bf16[16,8,1024]{2,1,0:T(8,128)(2,1)S(1)} %all_to_all.11.back_ref), custom_call_target="tpu_custom_call" | custom-call | tf_op jit(solution)/shard_map/restore/pallas_call | solution.py:225
Async XLA Ops:
  39.5 6.2 %collective-permute-start = (bf16[272,128]{1,0:T(8,128)(2,1)S(1)}, bf16[272,128]{1,0:T(8,128)(2,1)S(1)}, u32[]{:S(2)}, u32[]{:S(2)}) collective-permute-start(bf16[272,128]{1,0:T(8,128)(2,1)S(1)} %obs.1.sent_ref), channel_id=1, source_target_pairs={{0,1},{2,3},{4,5},{6,7},{8,9},{10,11},{12,13},{14,15},{31,30},{29,... | collective-permute-start | bytes 208904 | tf_op jit(solution)/shard_map/ppermute | solution.py:176
  42.8 5.6 %collective-permute-start.1 = (bf16[272,128]{1,0:T(8,128)(2,1)S(1)}, bf16[272,128]{1,0:T(8,128)(2,1)S(1)}, u32[]{:S(2)}, u32[]{:S(2)}) collective-permute-start(bf16[272,128]{1,0:T(8,128)(2,1)S(1)} %obs.1.sent_ref), channel_id=1, source_target_pairs={{1,2},{3,4},{5,6},{7,8},{9,10},{11,12},{13,14},{15,31},{30,29},{28... | collective-permute-start | bytes 208904 | tf_op jit(solution)/shard_map/ppermute | solution.py:176

commit v6 on v5

--- a/solution.py
+++ b/solution.py
@@ -1,3 +1,5 @@
+import functools
+
 import jax
 import jax.numpy as jnp
 from jax import lax
@@ -14,6 +16,7 @@
 LANES = 128
 CHUNK = 256
 POS_BASE = 32
+STRIDE = 1
 SENT_ROWS = 2 * MEMBERS + 16
 F32 = jnp.float32
 BF16 = jnp.bfloat16
@@ -24,13 +27,16 @@
     return pltpu.with_memory_space_constraint(x, pltpu.VMEM)
 
 
+def order_of(tiles):
+    return [(STRIDE * k) % tiles for k in range(tiles)]
+
+
 def place_of(tile, flipped, tiles):
     return tile + flipped * (tiles - 1 - 2 * tile)
 
 
-def spot_of(device, tiles):
-    flipped = lax.rem(lax.div(device, tiles), 2)
-    return place_of(lax.rem(device, tiles), flipped, tiles), flipped
+def tile_of(device, tiles):
+    return place_of(lax.rem(device, tiles), lax.rem(lax.div(device, tiles), 2), tiles)
 
 
 def prepare_kernel(
@@ -39,8 +45,9 @@
     count_ref, noise_ref, pick_ref, value_ref, error_ref, cell_ref, sem, small,
 ):
     tiles, mem_dev, _ = out_ref.shape
-    me, flipped = spot_of(lax.axis_index(("cell", "mem")), tiles)
-    places = [place_of(t, flipped, tiles) for t in range(tiles)]
+    me = tile_of(lax.axis_index(("cell", "mem")), tiles)
+    order = order_of(tiles)
+    slots = [order.index(t) for t in range(tiles)]
     inputs = (
         (noise_hbm, noise_ref),
         (pick_hbm, pick_ref),
@@ -55,7 +62,7 @@
     moved = [
         pltpu.make_async_copy(
             state_hbm.at[:, t * C_TILE : (t + 1) * C_TILE],
-            out_ref.at[places[t], :, 0:C_TILE],
+            out_ref.at[slots[t], :, 0:C_TILE],
             sem.at[t],
         )
         for t in range(tiles)
@@ -71,7 +78,7 @@
         value = jnp.take_along_axis(table[0], lane, axis=1)
         for k in range(1, len(table)):
             value = jnp.where(block == k, jnp.take_along_axis(table[k], lane, axis=1), value)
-        out_ref[places[t], :, C_TILE : C_TILE + OBS_CAP] = value.astype(BF16)
+        out_ref[slots[t], :, C_TILE : C_TILE + OBS_CAP] = value.astype(BF16)
     for copy in read[2:]:
         copy.wait()
     error = error_ref[pl.ds(me, 1), :]
@@ -81,7 +88,9 @@
     row_ref[1:2, :] = error
     row_ref[2:3, :] = jnp.sqrt(error)
     row_ref[3:4, :] = live.astype(F32)
-    row_ref[4:8, :] = jnp.zeros((4, OBS_CAP), F32)
+    edge = jnp.logical_or(me == 0, me == tiles - 1)
+    row_ref[4:5, :] = jnp.full((1, OBS_CAP), edge.astype(jnp.int32)).astype(F32)
+    row_ref[5:8, :] = jnp.zeros((3, OBS_CAP), F32)
     cells = lax.broadcasted_iota(jnp.int32, (C_TILE, OBS_CAP), 0)
     hot_ref[...] = (cells == cell).astype(F32).astype(BF16)
     row = lax.broadcasted_iota(jnp.int32, (16, OBS_CAP), 0)
@@ -92,15 +101,11 @@
 
 
 def restore_kernel(back_ref, out_ref, sem):
-    tiles = back_ref.shape[0]
-    _, flipped = spot_of(lax.axis_index(("cell", "mem")), tiles)
     moved = [
         pltpu.make_async_copy(
-            back_ref.at[place_of(t, flipped, tiles)],
-            out_ref.at[:, t * C_TILE : (t + 1) * C_TILE],
-            sem.at[t],
+            back_ref.at[k], out_ref.at[:, t * C_TILE : (t + 1) * C_TILE], sem.at[k]
         )
-        for t in range(tiles)
+        for k, t in enumerate(order_of(back_ref.shape[0]))
     ]
     for copy in moved:
         copy.start()
@@ -108,8 +113,26 @@
         copy.wait()
 
 
-def obs_kernel(tile_ref, hot_ref, row_ref, pos_ref, send_ref):
-    value, error, root, live = (row_ref[k : k + 1, :] for k in range(4))
+def restored(returned):
+    tiles, mem_dev, cells = returned.shape
+    return pl.pallas_call(
+        restore_kernel,
+        out_specs=ANY,
+        out_shape=jax.ShapeDtypeStruct((mem_dev, tiles * cells), BF16),
+        scratch_shapes=[pltpu.SemaphoreType.DMA((tiles,))],
+        name="restore",
+    )(here(returned))
+
+
+def in_other_order(x, tiles):
+    order = order_of(tiles)
+    size = MEMBERS // tiles
+    source = [order.index(tiles - 1 - t) for t in order]
+    return jnp.concatenate([x[k * size : (k + 1) * size, :] for k in source], axis=0)
+
+
+def obs_kernel(tile_ref, hot_ref, row_ref, pos_ref, near_ref, far_ref, *, tiles):
+    value, error, root, live, edge = (row_ref[k : k + 1, :] for k in range(5))
     at_obs = jnp.dot(tile_ref[:, 0:C_TILE], hot_ref[...], preferred_element_type=F32)
     perturb = tile_ref[:, C_TILE : C_TILE + OBS_CAP].astype(F32)
     mean_at = jnp.sum(at_obs, axis=0, keepdims=True) / MEMBERS
@@ -117,10 +140,14 @@
         MEMBERS - 1
     )
     weight = live / (spread + error)
+    obs_anom = (at_obs - mean_at) * live
     innovation = (value + root * perturb - at_obs) * weight
-    send_ref[0:MEMBERS, :] = ((at_obs - mean_at) * live).astype(BF16)
-    send_ref[MEMBERS : 2 * MEMBERS, :] = innovation.astype(BF16)
-    send_ref[2 * MEMBERS : SENT_ROWS, :] = pos_ref[...]
+    for k, rows in enumerate((obs_anom, innovation)):
+        cut = slice(k * MEMBERS, (k + 1) * MEMBERS)
+        near_ref[cut, :] = rows.astype(BF16)
+        far_ref[cut, :] = jnp.where(edge > 0.0, in_other_order(rows, tiles), rows).astype(BF16)
+    near_ref[2 * MEMBERS : SENT_ROWS, :] = pos_ref[...]
+    far_ref[2 * MEMBERS : SENT_ROWS, :] = pos_ref[...]
 
 
 def slots_of(sent_ref, side):
@@ -154,24 +181,41 @@
         out_ref[:, cut] = state + increment_of(anom, slots, start)
 
 
-def side_kernel(so_far_ref, anom_ref, near_ref, far_ref, out_ref):
-    near = slots_of(near_ref, 1)
-    far = slots_of(far_ref, -1)
+def side_kernel(so_far_ref, anom_ref, sent_ref, out_ref, *, side):
+    slots = slots_of(sent_ref, side)
     for start in range(0, C_TILE, CHUNK):
         cut = slice(start, start + CHUNK)
-        anom = anom_ref[:, cut]
-        total = so_far_ref[:, cut]
-        total = total + increment_of(anom, near, start) + increment_of(anom, far, start)
-        out_ref[:, cut] = total.astype(BF16)
+        total = so_far_ref[:, cut] + increment_of(anom_ref[:, cut], slots, start)
+        out_ref[:, cut] = total.astype(out_ref.dtype)
+
+
+def beside(so_far, anom, sent, side, dtype):
+    return pl.pallas_call(
+        functools.partial(side_kernel, side=side), out_shape=pltpu.VMEM((MEMBERS, C_TILE), dtype)
+    )(here(so_far), here(anom), here(sent))
+
+
+def line_of_tiles():
+    shards, tiles = lax.axis_size("cell"), lax.axis_size("mem")
+    return [
+        [shard * tiles + place_of(tile, shard % 2, tiles) for tile in range(tiles)]
+        for shard in range(shards)
+    ]
+
+
+def exchanged(x):
+    return lax.all_to_all(
+        x,
+        ("cell", "mem"),
+        split_axis=0,
+        concat_axis=0,
+        axis_index_groups=[[shard[t] for t in order_of(len(shard))] for shard in line_of_tiles()],
+        tiled=True,
+    )
 
 
 def swapped(x, first):
-    shards, tiles = lax.axis_size("cell"), lax.axis_size("mem")
-    line = [
-        shard * tiles + place_of(tile, shard % 2, tiles)
-        for shard in range(shards)
-        for tile in range(tiles)
-    ]
+    line = sum(line_of_tiles(), [])
     pairs = [(line[i], line[i + 1]) for i in range(first, len(line) - 1, 2)]
     return lax.ppermute(x, ("cell", "mem"), pairs + [(j, i) for i, j in pairs])
 
@@ -204,31 +248,29 @@
         obs_count, state, noise_table,
         rows(obs_noise), rows(obs_value), rows(obs_error), rows(obs_cell),
     )
-    tile = lax.all_to_all(packed, "mem", split_axis=0, concat_axis=0, tiled=True)
+    tile = exchanged(packed)
     tile = tile.reshape(MEMBERS, C_TILE + OBS_CAP)
-    sent = pl.pallas_call(
-        obs_kernel, out_shape=pltpu.VMEM((SENT_ROWS, OBS_CAP), BF16), name="obs"
+    sent, sent_far = pl.pallas_call(
+        functools.partial(obs_kernel, tiles=tiles),
+        out_shape=(pltpu.VMEM((SENT_ROWS, OBS_CAP), BF16),) * 2,
+        name="obs",
     )(here(tile), here(hot), here(numbers), here(digits))
-    far = swapped(sent, 1)
+    far = swapped(sent_far, 1)
     near = swapped(sent, 0)
     anom, so_far = pl.pallas_call(
         own_kernel,
-        out_shape=(pltpu.VMEM((MEMBERS, C_TILE), BF16), pltpu.VMEM((MEMBERS, C_TILE), F32)),
+        out_shape=(
+            pltpu.VMEM((MEMBERS, C_TILE), BF16),
+            pltpu.VMEM((MEMBERS, C_TILE), F32),
+        ),
         name="own",
     )(here(tile), here(sent))
-    analysis = pl.pallas_call(
-        side_kernel, out_shape=pltpu.VMEM((MEMBERS, C_TILE), BF16), name="side"
-    )(here(so_far), here(anom), here(near), here(far))
-    returned = lax.all_to_all(
-        analysis.reshape(tiles, mem_dev, C_TILE), "mem", split_axis=0, concat_axis=0, tiled=True
-    )
-    return pl.pallas_call(
-        restore_kernel,
-        out_specs=ANY,
-        out_shape=jax.ShapeDtypeStruct((mem_dev, cell_count), BF16),
-        scratch_shapes=[pltpu.SemaphoreType.DMA((tiles,))],
-        name="restore",
-    )(here(returned))
+    so_far = beside(so_far, anom, far, -1, F32)
+    analysis = beside(so_far, anom, near, 1, BF16)
+    returned = exchanged(analysis.reshape(tiles, mem_dev, C_TILE))
+    if order_of(tiles) != list(range(tiles)):
+        return restored(returned)
+    return jnp.transpose(returned, (1, 0, 2)).reshape(mem_dev, cell_count)
 
 
 def solution(mesh):

time: 74.7 us -> 73.2 us (0.980)
  the two profiles are of different devices: /device:TPU:20 before, /device:TPU:52 now
where the time goes in v6:
time: 73.2 us; the launch traced here: 72.9 us
  blocking collectives  61 us (83%)
  starting transfers between devices  6.19 us (8%)
  Pallas kernels  2.96 us (4%)
  waiting for transfers between devices  2.06 us (3%)
    all_to_all x2, blocking collectives, exchanged(): lax.all_to_all(x, ('cell', 'mem'), split_axis=0, concat_axis=0, axis_inde...  61 us
    ppermute x2, starting transfers between devices, swapped(): return lax.ppermute(x, ('cell', 'mem'), pairs + [(j, i) for i, j in pairs])  6.19 us
    ppermute x2, waiting for transfers between devices, swapped(): return lax.ppermute(x, ('cell', 'mem'), pairs + [(j, i) for i, j in pairs])  2.06 us
  transfers between devices with their start and end apart: 2, of which 1 were waited for; matrix products, arithmetic and copies ran while one was open for 0% of the time, Pallas kernels for 1%

profile of v6, /device:TPU:52, one launch (start us, length us, event | category | flops | bytes accessed | tf_op | source)
XLA Modules:
  0.0 72.9 jit_solution(5048594012880571553)
XLA Ops:
  0.0 1.3 %prepare.1 = (bf16[16,8,1152]{2,1,0:T(8,128)(2,1)S(1)}, bf16[1024,128]{1,0:T(8,128)(2,1)S(1)}, f32[8,128]{1,0:T(8,128)S(1)}, bf16[16,128]{1,0:T(8,128)(2,1)S(1)}) custom-call(s32[16]{0:T(128)} %count_hbm.1, bf16[8,16384]{1,0:T(8,128)(2,1)} %state_hbm.1, f32[8,512]{1,0:T(8,128)} %noise_hbm.1, s32[16,128]{1,0:T(8,128)} %bitcast.13, f32[16,128]{1,0:T(8,128)} %bitcast.14, ...), custom_call_target="tpu_custom_call" | custom-call | tf_op jit(solution)/shard_map/prepare/pallas_call | solution.py:227
  1.3 37.4 %all_to_all.10 = bf16[16,8,1152]{2,1,0:T(8,128)(2,1)S(1)} all-to-all(bf16[16,8,1152]{2,1,0:T(8,128)(2,1)S(1)} %get-tuple-element.13), channel_id=1, replica_groups={{0,1,2,3,4,5,6,7,8,9,10,11,12,13,14,15},{31,30,29,28,27,26,25,24,23,22,..., dimensions={0} | all-to-all | bytes 589824 | tf_op jit(solution)/shard_map/all_to_all | solution.py:207
  38.7 0.3 obs.1
  38.9 2.2 %collective-permute-start = (bf16[272,128]{1,0:T(8,128)(2,1)S(1)}, bf16[272,128]{1,0:T(8,128)(2,1)S(1)}, u32[]{:S(2)}, u32[]{:S(2)}) collective-permute-start(bf16[272,128]{1,0:T(8,128)(2,1)S(1)} %get-tuple-element.20), channel_id=1, source_target_pairs={{1,2},{3,4},{5,6},{7,8},{9,10},{11,12},{13,14},{15,31},{30,29},{28... | collective-permute-start | bytes 208904 | tf_op jit(solution)/shard_map/ppermute | solution.py:220
  41.1 4.0 %collective-permute-start.1 = (bf16[272,128]{1,0:T(8,128)(2,1)S(1)}, bf16[272,128]{1,0:T(8,128)(2,1)S(1)}, u32[]{:S(2)}, u32[]{:S(2)}) collective-permute-start(bf16[272,128]{1,0:T(8,128)(2,1)S(1)} %get-tuple-element.17.sent_ref), channel_id=1, source_target_pairs={{0,1},{2,3},{4,5},{6,7},{8,9},{10,11},{12,13},{14,15},{31,30},{29,... | collective-permute-start | bytes 208904 | tf_op jit(solution)/shard_map/ppermute | solution.py:220
  45.2 0.5 own.1
  45.6 0.0 collective-permute-done.sent_ref
  45.6 0.5 shard_map.73.so_far_ref
  46.1 2.1 %collective-permute-done.1.sent_ref = bf16[272,128]{1,0:T(8,128)(2,1)S(1)} collective-permute-done((bf16[272,128]{1,0:T(8,128)(2,1)S(1)}, bf16[272,128]{1,0:T(8,128)(2,1)S(1)}, u32[]{:S(2)}, u32[]{:S(2)}) %collective-permute-start.1) | collective-permute-done | bytes 69664 | tf_op jit(solution)/shard_map/ppermute | solution.py:220
  48.2 0.5 shard_map.74
  48.6 23.6 %all_to_all.11 = bf16[16,8,1024]{2,1,0:T(8,128)(2,1)S(1)} all-to-all(bf16[16,8,1024]{2,1,0:T(8,128)(2,1)S(1)} %bitcast.11), channel_id=1, replica_groups={{0,1,2,3,4,5,6,7,8,9,10,11,12,13,14,15},{31,30,29,28,27,26,25,24,23,22,..., dimensions={0} | all-to-all | bytes 524288 | tf_op jit(solution)/shard_map/all_to_all | solution.py:207
  72.2 0.7 copy.9
Async XLA Ops:
  38.9 6.7 %collective-permute-start = (bf16[272,128]{1,0:T(8,128)(2,1)S(1)}, bf16[272,128]{1,0:T(8,128)(2,1)S(1)}, u32[]{:S(2)}, u32[]{:S(2)}) collective-permute-start(bf16[272,128]{1,0:T(8,128)(2,1)S(1)} %get-tuple-element.20), channel_id=1, source_target_pairs={{1,2},{3,4},{5,6},{7,8},{9,10},{11,12},{13,14},{15,31},{30,29},{28... | collective-permute-start | bytes 208904 | tf_op jit(solution)/shard_map/ppermute | solution.py:220
  41.1 7.0 %collective-permute-start.1 = (bf16[272,128]{1,0:T(8,128)(2,1)S(1)}, bf16[272,128]{1,0:T(8,128)(2,1)S(1)}, u32[]{:S(2)}, u32[]{:S(2)}) collective-permute-start(bf16[272,128]{1,0:T(8,128)(2,1)S(1)} %get-tuple-element.17.sent_ref), channel_id=1, source_target_pairs={{0,1},{2,3},{4,5},{6,7},{8,9},{10,11},{12,13},{14,15},{31,30},{29,... | collective-permute-start | bytes 208904 | tf_op jit(solution)/shard_map/ppermute | solution.py:220

commit v7 on v6

--- a/solution.py
+++ b/solution.py
@@ -57,7 +57,7 @@
         (count_hbm, count_ref),
     )
     read = [pltpu.make_async_copy(a, b, small.at[k]) for k, (a, b) in enumerate(inputs)]
-    for copy in read:
+    for copy in read[:2]:
         copy.start()
     moved = [
         pltpu.make_async_copy(
@@ -67,14 +67,14 @@
         )
         for t in range(tiles)
     ]
-    for copy in moved:
+    for copy in moved + read[2:]:
         copy.start()
     for copy in read[:2]:
         copy.wait()
     table = [noise_ref[:, k * LANES : (k + 1) * LANES] for k in range(NOISE // LANES)]
     for t in range(tiles):
         index = jnp.broadcast_to(pick_ref[t : t + 1, :], (mem_dev, OBS_CAP))
-        lane, block = index % LANES, index // LANES
+        lane, block = jnp.bitwise_and(index, LANES - 1), lax.shift_right_logical(index, LANES.bit_length() - 1)
         value = jnp.take_along_axis(table[0], lane, axis=1)
         for k in range(1, len(table)):
             value = jnp.where(block == k, jnp.take_along_axis(table[k], lane, axis=1), value)
@@ -90,11 +90,15 @@
     row_ref[3:4, :] = live.astype(F32)
     edge = jnp.logical_or(me == 0, me == tiles - 1)
     row_ref[4:5, :] = jnp.full((1, OBS_CAP), edge.astype(jnp.int32)).astype(F32)
-    row_ref[5:8, :] = jnp.zeros((3, OBS_CAP), F32)
+    odd = lax.rem(me, 2)
+    above = cell_ref[pl.ds(me + 1 - 2 * odd, 1), :] + C_TILE * (1 - 2 * odd)
+    row_ref[5:6, :] = above.astype(F32)
+    row_ref[6:7, :] = cell.astype(F32)
+    row_ref[7:8, :] = jnp.zeros((1, OBS_CAP), F32)
     cells = lax.broadcasted_iota(jnp.int32, (C_TILE, OBS_CAP), 0)
     hot_ref[...] = (cells == cell).astype(F32).astype(BF16)
     row = lax.broadcasted_iota(jnp.int32, (16, OBS_CAP), 0)
-    digits = jnp.where(row == 0, cell // POS_BASE, cell % POS_BASE)
+    digits = jnp.where(row == 0, lax.div(cell, POS_BASE), lax.rem(cell, POS_BASE))
     pos_ref[...] = jnp.where(row == 2, lax.rem(me, 2), digits).astype(F32).astype(BF16)
     for copy in moved:
         copy.wait()
@@ -146,53 +150,61 @@
         cut = slice(k * MEMBERS, (k + 1) * MEMBERS)
         near_ref[cut, :] = rows.astype(BF16)
         far_ref[cut, :] = jnp.where(edge > 0.0, in_other_order(rows, tiles), rows).astype(BF16)
-    near_ref[2 * MEMBERS : SENT_ROWS, :] = pos_ref[...]
     far_ref[2 * MEMBERS : SENT_ROWS, :] = pos_ref[...]
 
 
-def slots_of(sent_ref, side):
+def column(row):
+    square = jnp.transpose(jnp.broadcast_to(row, (OBS_CAP, OBS_CAP)))
+    return jnp.concatenate([square] * (CHUNK // OBS_CAP), axis=1)
+
+
+def far_position(sent_ref):
     digits = sent_ref[2 * MEMBERS : SENT_ROWS, :].astype(F32)
-    shift = (2.0 * digits[2:3, :] - 1.0) * float(side * C_TILE)
-    position = digits[0:1, :] * POS_BASE + digits[1:2, :] + shift
-    position = jnp.transpose(jnp.broadcast_to(position, (OBS_CAP, OBS_CAP)))
-    wide = jnp.concatenate([position] * (CHUNK // OBS_CAP), axis=1)
-    return sent_ref[0:MEMBERS, :], sent_ref[MEMBERS : 2 * MEMBERS, :], wide
-
-
-def increment_of(anom, slots, start):
-    obs_anom, innovation, position = slots
-    covariance = lax.dot_general(
-        obs_anom, anom, (((0,), (0,)), ((), ())), preferred_element_type=F32
-    )
+    shift = (1.0 - 2.0 * digits[2:3, :]) * float(C_TILE)
+    return column(digits[0:1, :] * POS_BASE + digits[1:2, :] + shift)
+
+
+def taper_of(position, start):
     cells = lax.broadcasted_iota(jnp.int32, (OBS_CAP, CHUNK), 1).astype(F32) + float(start)
     away = cells - position
     inner = jnp.maximum(1.0 - (away * away) * (1.0 / (LOCALIZE * LOCALIZE)), 0.0)
-    gain = (inner * inner * (covariance * (1.0 / (MEMBERS - 1)))).astype(BF16)
-    return jnp.dot(innovation, gain, preferred_element_type=F32)
-
-
-def own_kernel(tile_ref, sent_ref, anom_ref, out_ref):
-    slots = slots_of(sent_ref, 0)
-    for start in range(0, C_TILE, CHUNK):
-        cut = slice(start, start + CHUNK)
+    return inner * inner * (1.0 / (MEMBERS - 1))
+
+
+def increment_of(anom, sent_ref, taper):
+    covariance = lax.dot_general(
+        sent_ref[0:MEMBERS, :], anom, (((0,), (0,)), ((), ())), preferred_element_type=F32
+    )
+    gain = (taper * covariance).astype(BF16)
+    return jnp.dot(sent_ref[MEMBERS : 2 * MEMBERS, :], gain, preferred_element_type=F32)
+
+
+STRETCHES = [(start, slice(start, start + CHUNK)) for start in range(0, C_TILE, CHUNK)]
+
+
+def own_kernel(tile_ref, sent_ref, row_ref, anom_ref, out_ref, taper_ref):
+    position = column(row_ref[6:7, :])
+    for start, cut in STRETCHES:
         state = tile_ref[:, cut].astype(F32)
         anom = (state - jnp.sum(state, axis=0, keepdims=True) / MEMBERS).astype(BF16)
         anom_ref[:, cut] = anom
-        out_ref[:, cut] = state + increment_of(anom, slots, start)
-
-
-def side_kernel(so_far_ref, anom_ref, sent_ref, out_ref, *, side):
-    slots = slots_of(sent_ref, side)
-    for start in range(0, C_TILE, CHUNK):
-        cut = slice(start, start + CHUNK)
-        total = so_far_ref[:, cut] + increment_of(anom_ref[:, cut], slots, start)
-        out_ref[:, cut] = total.astype(out_ref.dtype)
-
-
-def beside(so_far, anom, sent, side, dtype):
-    return pl.pallas_call(
-        functools.partial(side_kernel, side=side), out_shape=pltpu.VMEM((MEMBERS, C_TILE), dtype)
-    )(here(so_far), here(anom), here(sent))
+        out_ref[:, cut] = state + increment_of(anom, sent_ref, taper_of(position, start))
+    position = column(row_ref[5:6, :])
+    for start, cut in STRETCHES:
+        taper_ref[:, cut] = taper_of(position, start)
+
+
+def far_kernel(so_far_ref, anom_ref, sent_ref, out_ref):
+    position = far_position(sent_ref)
+    for start, cut in STRETCHES:
+        part = increment_of(anom_ref[:, cut], sent_ref, taper_of(position, start))
+        out_ref[:, cut] = so_far_ref[:, cut] + part
+
+
+def near_kernel(so_far_ref, anom_ref, taper_ref, sent_ref, out_ref):
+    for _, cut in STRETCHES:
+        part = increment_of(anom_ref[:, cut], sent_ref, taper_ref[:, cut])
+        out_ref[:, cut] = (so_far_ref[:, cut] + part).astype(BF16)
 
 
 def line_of_tiles():
@@ -252,21 +264,29 @@
     tile = tile.reshape(MEMBERS, C_TILE + OBS_CAP)
     sent, sent_far = pl.pallas_call(
         functools.partial(obs_kernel, tiles=tiles),
-        out_shape=(pltpu.VMEM((SENT_ROWS, OBS_CAP), BF16),) * 2,
+        out_shape=(
+            pltpu.VMEM((2 * MEMBERS, OBS_CAP), BF16),
+            pltpu.VMEM((SENT_ROWS, OBS_CAP), BF16),
+        ),
         name="obs",
     )(here(tile), here(hot), here(numbers), here(digits))
     far = swapped(sent_far, 1)
     near = swapped(sent, 0)
-    anom, so_far = pl.pallas_call(
+    anom, so_far, taper = pl.pallas_call(
         own_kernel,
         out_shape=(
             pltpu.VMEM((MEMBERS, C_TILE), BF16),
             pltpu.VMEM((MEMBERS, C_TILE), F32),
+            pltpu.VMEM((OBS_CAP, C_TILE), F32),
         ),
         name="own",
-    )(here(tile), here(sent))
-    so_far = beside(so_far, anom, far, -1, F32)
-    analysis = beside(so_far, anom, near, 1, BF16)
+    )(here(tile), here(sent), here(numbers))
+    so_far = pl.pallas_call(
+        far_kernel, out_shape=pltpu.VMEM((MEMBERS, C_TILE), F32), name="far"
+    )(here(so_far), here(anom), here(far))
+    analysis = pl.pallas_call(
+        near_kernel, out_shape=pltpu.VMEM((MEMBERS, C_TILE), BF16), name="near"
+    )(here(so_far), here(anom), here(taper), here(near))
     returned = exchanged(analysis.reshape(tiles, mem_dev, C_TILE))
     if order_of(tiles) != list(range(tiles)):
         return restored(returned)

time: 73.2 us -> 73.2 us (level)
  the two profiles are of different devices: /device:TPU:52 before, /device:TPU:46 now
where the time goes in v7:
time: 73.2 us; the launch traced here: 72.9 us
  blocking collectives  61.5 us (84%)
  starting transfers between devices  6.18 us (8%)
  Pallas kernels  2.98 us (4%)
  waiting for transfers between devices  1.45 us (2%)
    all_to_all x2, blocking collectives, exchanged(): lax.all_to_all(x, ('cell', 'mem'), split_axis=0, concat_axis=0, axis_inde...  61.5 us
    ppermute x2, starting transfers between devices, swapped(): return lax.ppermute(x, ('cell', 'mem'), pairs + [(j, i) for i, j in pairs])  6.18 us
  transfers between devices with their start and end apart: 2, of which 1 were waited for; matrix products, arithmetic and copies ran while one was open for 0% of the time, Pallas kernels for 1%

profile of v7, /device:TPU:46, one launch (start us, length us, event | category | flops | bytes accessed | tf_op | source)
XLA Modules:
  0.0 72.9 jit_solution(627175925903169)
XLA Ops:
  0.0 1.3 %prepare.1 = (bf16[16,8,1152]{2,1,0:T(8,128)(2,1)S(1)}, bf16[1024,128]{1,0:T(8,128)(2,1)S(1)}, f32[8,128]{1,0:T(8,128)S(1)}, bf16[16,128]{1,0:T(8,128)(2,1)S(1)}) custom-call(s32[16]{0:T(128)} %count_hbm.1, bf16[8,16384]{1,0:T(8,128)(2,1)} %state_hbm.1, f32[8,512]{1,0:T(8,128)} %noise_hbm.1, s32[16,128]{1,0:T(8,128)} %bitcast.13, f32[16,128]{1,0:T(8,128)} %bitcast.14, ...), custom_call_target="tpu_custom_call" | custom-call | tf_op jit(solution)/shard_map/prepare/pallas_call | solution.py:239
  1.3 37.4 %all_to_all.10 = bf16[16,8,1152]{2,1,0:T(8,128)(2,1)S(1)} all-to-all(bf16[16,8,1152]{2,1,0:T(8,128)(2,1)S(1)} %get-tuple-element.14), channel_id=1, replica_groups={{0,1,2,3,4,5,6,7,8,9,10,11,12,13,14,15},{31,30,29,28,27,26,25,24,23,22,..., dimensions={0} | all-to-all | bytes 589824 | tf_op jit(solution)/shard_map/all_to_all | solution.py:219
  38.7 0.3 obs.1
  38.9 2.5 %collective-permute-start = (bf16[272,128]{1,0:T(8,128)(2,1)S(1)}, bf16[272,128]{1,0:T(8,128)(2,1)S(1)}, u32[]{:S(2)}, u32[]{:S(2)}) collective-permute-start(bf16[272,128]{1,0:T(8,128)(2,1)S(1)} %get-tuple-element.21), channel_id=1, source_target_pairs={{1,2},{3,4},{5,6},{7,8},{9,10},{11,12},{13,14},{15,31},{30,29},{28... | collective-permute-start | bytes 208904 | tf_op jit(solution)/shard_map/ppermute | solution.py:232
  41.4 3.7 %collective-permute-start.1 = (bf16[256,128]{1,0:T(8,128)(2,1)S(1)}, bf16[256,128]{1,0:T(8,128)(2,1)S(1)}, u32[]{:S(2)}, u32[]{:S(2)}) collective-permute-start(bf16[256,128]{1,0:T(8,128)(2,1)S(1)} %get-tuple-element.18.sent_ref), channel_id=1, source_target_pairs={{0,1},{2,3},{4,5},{6,7},{8,9},{10,11},{12,13},{14,15},{31,30},{29,... | collective-permute-start | bytes 196616 | tf_op jit(solution)/shard_map/ppermute | solution.py:232
  45.1 0.5 own.1
  45.7 0.0 collective-permute-done.sent_ref
  45.7 0.5 far.1.so_far_ref
  46.1 1.5 %collective-permute-done.1.sent_ref = bf16[256,128]{1,0:T(8,128)(2,1)S(1)} collective-permute-done((bf16[256,128]{1,0:T(8,128)(2,1)S(1)}, bf16[256,128]{1,0:T(8,128)(2,1)S(1)}, u32[]{:S(2)}, u32[]{:S(2)}) %collective-permute-start.1) | collective-permute-done | bytes 65568 | tf_op jit(solution)/shard_map/ppermute | solution.py:232
  47.6 0.5 near.1
  48.0 24.1 %all_to_all.11 = bf16[16,8,1024]{2,1,0:T(8,128)(2,1)S(1)} all-to-all(bf16[16,8,1024]{2,1,0:T(8,128)(2,1)S(1)} %bitcast.11), channel_id=1, replica_groups={{0,1,2,3,4,5,6,7,8,9,10,11,12,13,14,15},{31,30,29,28,27,26,25,24,23,22,..., dimensions={0} | all-to-all | bytes 524288 | tf_op jit(solution)/shard_map/all_to_all | solution.py:219
  72.2 0.7 copy.9
Async XLA Ops:
  38.9 6.7 %collective-permute-start = (bf16[272,128]{1,0:T(8,128)(2,1)S(1)}, bf16[272,128]{1,0:T(8,128)(2,1)S(1)}, u32[]{:S(2)}, u32[]{:S(2)}) collective-permute-start(bf16[272,128]{1,0:T(8,128)(2,1)S(1)} %get-tuple-element.21), channel_id=1, source_target_pairs={{1,2},{3,4},{5,6},{7,8},{9,10},{11,12},{13,14},{15,31},{30,29},{28... | collective-permute-start | bytes 208904 | tf_op jit(solution)/shard_map/ppermute | solution.py:232
  41.4 6.2 %collective-permute-start.1 = (bf16[256,128]{1,0:T(8,128)(2,1)S(1)}, bf16[256,128]{1,0:T(8,128)(2,1)S(1)}, u32[]{:S(2)}, u32[]{:S(2)}) collective-permute-start(bf16[256,128]{1,0:T(8,128)(2,1)S(1)} %get-tuple-element.18.sent_ref), channel_id=1, source_target_pairs={{0,1},{2,3},{4,5},{6,7},{8,9},{10,11},{12,13},{14,15},{31,30},{29,... | collective-permute-start | bytes 196616 | tf_op jit(solution)/shard_map/ppermute | solution.py:232
